TPU v7x, 256 devices: a whole 4x4x8 slice. The times are simulated.
256 devices in a mesh: pl: 16 (over y, x), xs: 16 (over z, core).
Axes of the slice: x: 4, y: 4, z: 8, core: 2. Of those that a mesh axis runs over, the one named last changes fastest.
Arguments:
- source: float32 [512, 16, 2048], P('xs', None, 'pl'), may hold values from -6 to 6
- eastward_rate: float32 [512, 16, 2048], P('xs', None, 'pl'), may hold values from 300 to 6000
- northward_rate: float32 [512, 16, 2048], P('xs', None, 'pl'), may hold values from 300 to 6000
- vertical_rate: float32 [512, 16, 2048], P('xs', None, 'pl'), may hold values from 0.5 to 20
- amplitude: float32 [512, 16, 2048], P('xs', None, 'pl'), may hold values from 300 to 3000
Outputs:
- smoothed: float32 [512, 16, 2048], P('xs', None, 'pl')
All inputs are finite; a program needn't handle non-finite values.
Results may differ from a plain program's by a relative error of at most 0.0003.
Values sent between devices are 32-bit elements; how exact they have to be, the bound alone decides.
A program may use at most 128 MiB of HBM per device.

v0:
```python
import jax
import jax.numpy as jnp
from jax import lax
from jax.sharding import PartitionSpec as P


def cyclic(sub_band, centre, super_band, values):
    length = centre.shape[0]
    if length == 1:
        return values / centre

    def halves(operand):
        paired = operand.reshape((length // 2, 2) + operand.shape[1:])
        return (paired[:, 0], paired[:, 1])

    def following(operand, filler):
        return jnp.concatenate([operand[1:], jnp.full_like(operand[:1], filler)], axis=0)

    sub_even, sub_odd = halves(sub_band)
    centre_even, centre_odd = halves(centre)
    super_even, super_odd = halves(super_band)
    values_even, values_odd = halves(values)
    left_factor = -sub_odd / centre_even
    right_factor = -super_odd / following(centre_even, 1.0)
    reduced = cyclic(
        left_factor * sub_even,
        centre_odd + left_factor * super_even + right_factor * following(sub_even, 0.0),
        right_factor * following(super_even, 0.0),
        values_odd + left_factor * values_even + right_factor * following(values_even, 0.0),
    )
    previous = jnp.concatenate([jnp.zeros_like(reduced[:1]), reduced[:-1]], axis=0)
    even_part = (values_even - sub_even * previous - super_even * reduced) / centre_even
    return jnp.stack([even_part, reduced], axis=1).reshape((length,) + even_part.shape[1:])


def cyclic_last(sub_band, centre, super_band, values):
    length = centre.shape[-1]
    if length == 1:
        return values / centre

    def halves(operand):
        paired = operand.reshape(operand.shape[:-1] + (length // 2, 2))
        return (paired[..., 0], paired[..., 1])

    def following(operand, filler):
        return jnp.concatenate([operand[..., 1:], jnp.full_like(operand[..., :1], filler)], axis=-1)

    sub_even, sub_odd = halves(sub_band)
    centre_even, centre_odd = halves(centre)
    super_even, super_odd = halves(super_band)
    values_even, values_odd = halves(values)
    left_factor = -sub_odd / centre_even
    right_factor = -super_odd / following(centre_even, 1.0)
    reduced = cyclic_last(
        left_factor * sub_even,
        centre_odd + left_factor * super_even + right_factor * following(sub_even, 0.0),
        right_factor * following(super_even, 0.0),
        values_odd + left_factor * values_even + right_factor * following(values_even, 0.0),
    )
    previous = jnp.concatenate([jnp.zeros_like(reduced[..., :1]), reduced[..., :-1]], axis=-1)
    even_part = (values_even - sub_even * previous - super_even * reduced) / centre_even
    return jnp.stack([even_part, reduced], axis=-1).reshape(even_part.shape[:-1] + (length,))


def band_solve(values, rate_lines):
    length = values.shape[0]
    position = lax.broadcasted_iota(jnp.int32, rate_lines.shape, 0)
    sub_band = jnp.where(position > 0, -rate_lines, 0.0)
    super_band = jnp.where(position < length - 1, -rate_lines, 0.0)
    return cyclic(sub_band, 1.0 + 2.0 * rate_lines, super_band, values)


def vertical_solve(values, vertical_lines):
    return jnp.moveaxis(band_solve(jnp.moveaxis(values, 1, 0), vertical_lines), 0, 1)


def northward_solve(values, north_lines):
    length = values.shape[-1]
    position = lax.broadcasted_iota(jnp.int32, north_lines.shape, 2)
    sub_band = jnp.where(position > 0, -north_lines, 0.0)
    super_band = jnp.where(position < length - 1, -north_lines, 0.0)
    return cyclic_last(sub_band, 1.0 + 2.0 * north_lines, super_band, values)


def to_lines(values):
    return lax.all_to_all(values, "pl", split_axis=1, concat_axis=2, tiled=True)


def to_planes(values):
    return lax.all_to_all(values, "pl", split_axis=2, concat_axis=1, tiled=True)


def matrix_product(left_matrix, right_matrix):
    return (
        left_matrix[0] * right_matrix[0] + left_matrix[1] * right_matrix[2],
        left_matrix[0] * right_matrix[1] + left_matrix[1] * right_matrix[3],
        left_matrix[2] * right_matrix[0] + left_matrix[3] * right_matrix[2],
        left_matrix[2] * right_matrix[1] + left_matrix[3] * right_matrix[3],
    )


def matrix_inverse(matrix):
    determinant = matrix[0] * matrix[3] - matrix[1] * matrix[2]
    return (
        matrix[3] / determinant,
        -matrix[1] / determinant,
        -matrix[2] / determinant,
        matrix[0] / determinant,
    )


def matrix_vector(matrix, vector):
    return (
        matrix[0] * vector[0] + matrix[1] * vector[1],
        matrix[2] * vector[0] + matrix[3] * vector[1],
    )


def unpack_rows(packed):
    sub_block = (packed[0], packed[1], packed[2], packed[3])
    centre = (packed[4] + 1.0, packed[5], packed[6], packed[7] + 1.0)
    super_block = (packed[8], packed[9], packed[10], packed[11])
    right_side = (packed[12], packed[13])
    return (sub_block, centre, super_block, right_side)


def pack_rows(sub_block, centre, super_block, right_side):
    return jnp.stack(
        [
            sub_block[0],
            sub_block[1],
            sub_block[2],
            sub_block[3],
            centre[0] - 1.0,
            centre[1],
            centre[2],
            centre[3] - 1.0,
            super_block[0],
            super_block[1],
            super_block[2],
            super_block[3],
            right_side[0],
            right_side[1],
        ]
    )


def first_rows(boundary):
    blank_rows = jnp.zeros_like(boundary[0])
    return jnp.stack(
        [
            blank_rows,
            boundary[0],
            blank_rows,
            boundary[1],
            blank_rows,
            blank_rows,
            blank_rows,
            blank_rows,
            boundary[2],
            blank_rows,
            boundary[3],
            blank_rows,
            boundary[4],
            boundary[5],
        ]
    )


def eliminate(own_rows, rows_below, rows_above):
    sub_block, centre, super_block, right_side = unpack_rows(own_rows)
    sub_below, centre_below, super_below, right_below = unpack_rows(rows_below)
    sub_above, centre_above, super_above, right_above = unpack_rows(rows_above)
    left_factor = matrix_product(sub_block, matrix_inverse(centre_below))
    right_factor = matrix_product(super_block, matrix_inverse(centre_above))
    new_sub = tuple((-entry for entry in matrix_product(left_factor, sub_below)))
    new_super = tuple((-entry for entry in matrix_product(right_factor, super_above)))
    left_part = matrix_product(left_factor, super_below)
    right_part = matrix_product(right_factor, sub_above)
    new_centre = tuple((centre[slot] - left_part[slot] - right_part[slot] for slot in range(4)))
    left_vector = matrix_vector(left_factor, right_below)
    right_vector = matrix_vector(right_factor, right_above)
    new_right = (
        right_side[0] - left_vector[0] - right_vector[0],
        right_side[1] - left_vector[1] - right_vector[1],
    )
    return pack_rows(new_sub, new_centre, new_super, new_right)


def finish_rows(packed):
    sub_block, centre, super_block, right_side = unpack_rows(packed)
    return matrix_vector(matrix_inverse(centre), right_side)


def solve_gathered(gathered, own_index, devices):
    row_blocks = first_rows(jnp.moveaxis(gathered, 0, 1))
    stride = 1
    while stride < devices:
        blank_rows = jnp.zeros_like(row_blocks[:, :stride])
        rows_below = jnp.concatenate([blank_rows, row_blocks[:, :-stride]], axis=1)
        rows_above = jnp.concatenate([row_blocks[:, stride:], blank_rows], axis=1)
        row_blocks = eliminate(row_blocks, rows_below, rows_above)
        stride = stride * 2
    first_value, last_value = finish_rows(row_blocks)
    blank_value = jnp.zeros_like(first_value[:1])
    padded_first = jnp.concatenate([blank_value, first_value, blank_value], axis=0)
    padded_last = jnp.concatenate([blank_value, last_value, blank_value], axis=0)
    last_before = lax.dynamic_index_in_dim(padded_last, own_index, 0, keepdims=False)
    first_after = lax.dynamic_index_in_dim(padded_first, own_index + 2, 0, keepdims=False)
    return (last_before, first_after)


def coupled(boundary):
    devices = lax.axis_size("xs")
    gathered = lax.all_gather(boundary[None], "xs", axis=0, tiled=True)
    last_before, first_after = solve_gathered(gathered, lax.axis_index("xs"), devices)
    return (last_before, first_after)


def spike_parts(values, rate, own_index, devices):
    length = values.shape[0]
    position = lax.broadcasted_iota(jnp.int32, values.shape, 0)
    sub_band = jnp.where(position > 0, -rate, 0.0)
    super_band = jnp.where(position < length - 1, -rate, 0.0)
    centre = 1.0 + 2.0 * rate
    left_edge = jnp.where((position == 0) & (own_index > 0), -rate, 0.0)
    right_edge = jnp.where((position == length - 1) & (own_index < devices - 1), -rate, 0.0)
    stacked = jnp.stack([values, left_edge, right_edge], axis=1)
    solved = cyclic(sub_band[:, None], centre[:, None], super_band[:, None], stacked)
    particular = solved[:, 0]
    spike_left = solved[:, 1]
    spike_right = solved[:, 2]
    boundary = jnp.stack(
        [
            spike_left[0],
            spike_left[-1],
            spike_right[0],
            spike_right[-1],
            particular[0],
            particular[-1],
        ]
    )
    return (particular, spike_left, spike_right, boundary)


def eastward_solve(values, east_rate):
    particular, spike_left, spike_right, boundary = spike_parts(
        values, east_rate, lax.axis_index("xs"), lax.axis_size("xs")
    )
    last_before, first_after = coupled(boundary)
    return particular - spike_left * last_before[None] - spike_right * first_after[None]


def shards(source, eastward_rate, northward_rate, vertical_rate, amplitude):
    vertical_lines = jnp.moveaxis(vertical_rate, 1, 0)
    values = vertical_solve(source, vertical_lines)
    north_lines = lax.all_to_all(northward_rate, "pl", split_axis=1, concat_axis=2, tiled=True)
    values = to_planes(northward_solve(to_lines(values), north_lines))
    values = eastward_solve(values, eastward_rate)
    values = eastward_solve(values, eastward_rate)
    values = to_planes(northward_solve(to_lines(values), north_lines))
    values = vertical_solve(values, vertical_lines)
    return amplitude * values


def solution(mesh):
    placed = (
        P("xs", None, "pl"),
        P("xs", None, "pl"),
        P("xs", None, "pl"),
        P("xs", None, "pl"),
        P("xs", None, "pl"),
    )
    return jax.shard_map(
        shards, mesh=mesh, in_specs=placed, out_specs=P("xs", None, "pl"), check_vma=False
    )
```

profile of v0, /device:TPU:32, one launch (start us, length us, event | category | flops | bytes accessed | tf_op | source)
XLA Modules:
  0.0 218.9 jit_solution(4738351005885732317)
XLA Ops:
  3.7 7.0 %all-to-all-start = ((f32[32,16,128]{2,0,1:T(8,128)}), f32[32,16,128]{2,0,1:T(8,128)S(1)}, u32[]{:S(2)}, u32[]{:S(2)}) async-start(f32[32,16,128]{2,0,1:T(8,128)} %bitcast.68), calls=%async_computation | async-start | bytes 524288 | tf_op jit(solution)/shard_map/all_to_all | solution.py:86
  27.6 7.4 %all-to-all-start.1 = ((f32[32,16,128]{2,0,1:T(8,128)}), f32[32,16,128]{2,0,1:T(8,128)S(1)}, u32[]{:S(2)}, u32[]{:S(2)}) async-start(f32[32,16,128]{2,0,1:T(8,128)} %copy.1550), calls=%async_computation.1 | async-start | bytes 524288 | tf_op jit(solution)/shard_map/all_to_all | solution.py:257
  35.3 1.6 fusion.580
  37.8 5.9 %all-to-all-done.1 = f32[32,16,128]{2,0,1:T(8,128)S(1)} async-done(((f32[32,16,128]{2,0,1:T(8,128)}), f32[32,16,128]{2,0,1:T(8,128)S(1)}, u32[]{:S(2)}, u32[]{:S(2)}) %all-to-all-start.1) | async-done | bytes 262176 | tf_op jit(solution)/shard_map/all_to_all | solution.py:257
  44.1 1.6 fusion.579
  47.2 2.6 %copy_select_fusion = (f32[32,1,1024,2]{0,2,3,1:T(8,128)S(1)}, f32[32,1,1024,2]{0,2,3,1:T(8,128)S(1)}) fusion(f32[32,1,1024,2]{0,3,2,1:T(2,128)} %bitcast.4710, pred[1024,2]{0,1:T(4,128)(4,1)S(1)} %get-tuple-element.502, pred[1024,2]{0,1:T(4,128)(4,1)S(1)} %get-tuple-element.503), kind=kLoop, calls=%fused_computation.210 | loop fusion | flops 131072 | bytes 790528 | tf_op jit(solution)/shard_map/jit(_where)/select_n | solution.py:81
  61.8 1.9 copy.1628
  64.2 11.6 %reduce = f32[2048,32]{1,0:T(8,128)} reduce(f32[2048,1,32]{2,1,0:T(1,128)} %bitcast.4714, f32[]{:T(128)} %broadcast.2033), dimensions={1}, to_apply=%bitcast.4048.reduce_sub_computation | reduce | bytes 524292
  75.8 2.4 %reshape.3598 = f32[16,1,4096]{2,1,0:T(1,128)} reshape(f32[2048,32]{1,0:T(8,128)} %reduce) | data formatting | bytes 524288
  78.2 4.2 %all-to-all-start.2 = ((f32[16,1,4096]{2,1,0:T(1,128)}), f32[16,1,4096]{2,1,0:T(1,128)}, u32[]{:S(2)}, u32[]{:S(2)}) async-start(f32[16,1,4096]{2,1,0:T(1,128)} %reshape.3598), calls=%async_computation.2 | async-start | bytes 524288 | tf_op jit(solution)/shard_map/all_to_all | solution.py:90
  85.1 1.8 bitcast_divide_fusion.61
  86.9 4.2 %all-to-all-done.2 = f32[16,1,4096]{2,1,0:T(1,128)} async-done(((f32[16,1,4096]{2,1,0:T(1,128)}), f32[16,1,4096]{2,1,0:T(1,128)}, u32[]{:S(2)}, u32[]{:S(2)}) %all-to-all-start.2) | async-done | bytes 262176 | tf_op jit(solution)/shard_map/all_to_all | solution.py:90
  91.1 2.9 %reduce.1 = f32[16,4096]{1,0:T(8,128)} reduce(f32[16,1,4096]{2,1,0:T(1,128)} %all-to-all-done.2, f32[]{:T(128)} %broadcast.2033), dimensions={1}, to_apply=%all_to_all.14.reduce_sub_computation | reduce | bytes 524292 | tf_op jit(solution)/shard_map/all_to_all | solution.py:90
  93.9 3.7 %reshape.3599 = f32[2048,1,32]{2,1,0:T(1,128)} reshape(f32[16,4096]{1,0:T(8,128)} %reduce.1) | data formatting | bytes 524288
  97.7 3.4 %copy.1630 = f32[32,1,2048]{2,1,0:T(1,128)} copy(f32[32,1,2048]{0,1,2:T(1,128)} %bitcast.4711) | data formatting | bytes 524288 | tf_op jit(solution)/shard_map/all_to_all | solution.py:90
  104.9 20.5 %all-gather = f32[96,16,128]{2,1,0:T(8,128)S(1)} all-gather(f32[6,16,128]{2,1,0:T(8,128)S(1)} %constant_dynamic-update-slice_fusion), channel_id=2, replica_groups=mesh['pl'=16,'xs'=16] {'xs'}, dimensions={0}, use_global_device_ids=true | all-gather | bytes 835584 | tf_op jit(solution)/shard_map/all_gather | solution.py:215
  130.9 5.1 %fusion.406 = (f32[16,16,128]{2,1,0:T(8,128)S(1)}, f32[16,16,128]{2,1,0:T(8,128)S(1)}, f32[16,16,128]{2,1,0:T(8,128)S(1)}, f32[16,16,128]{2,1,0:T(8,128)S(1)}, f...) fusion(f32[16,16,128]{2,1,0:T(8,128)S(1)} %get-tuple-element.322, ...), kind=kLoop, calls=%fused_computation.1275 | loop fusion | flops 23101440 | bytes 16613376 | tf_op jit(solution)/shard_map/add | solution.py:115
  138.8 18.6 %all-gather.1 = f32[96,16,128]{2,1,0:T(8,128)S(1)} all-gather(f32[6,16,128]{2,1,0:T(8,128)S(1)} %constant_dynamic-update-slice_fusion.56), channel_id=3, replica_groups=mesh['pl'=16,'xs'=16] {'xs'}, dimensions={0}, use_global_device_ids=true | all-gather | bytes 835584 | tf_op jit(solution)/shard_map/all_gather | solution.py:215
  162.9 5.0 %fusion.403 = (f32[16,16,128]{2,1,0:T(8,128)S(1)}, f32[16,16,128]{2,1,0:T(8,128)S(1)}, f32[16,16,128]{2,1,0:T(8,128)S(1)}, f32[16,16,128]{2,1,0:T(8,128)S(1)}, f...) fusion(f32[16,16,128]{2,1,0:T(8,128)S(1)} %get-tuple-element.316, ...), kind=kLoop, calls=%fused_computation.1183 | loop fusion | flops 23101440 | bytes 16613376 | tf_op jit(solution)/shard_map/add | solution.py:115
  168.2 12.3 %all_to_all.23 = f32[32,16,128]{2,0,1:T(8,128)S(1)} all-to-all(f32[32,16,128]{2,0,1:T(8,128)S(1)} %copy.1714), channel_id=1, replica_groups=mesh['pl'=16,'xs'=16] {'pl'}, dimensions={1} | all-to-all | bytes 524288 | tf_op jit(solution)/shard_map/all_to_all | solution.py:86
  181.8 2.5 %fusion.578 = (f32[32,1,1024,1]{0,3,2,1:T(1,128)S(1)}, f32[32,1,1024,1]{0,3,2,1:T(1,128)S(1)}) fusion(f32[32,1,1024,2]{0,3,2,1:T(2,128)} %bitcast.4715), kind=kLoop, calls=%fused_computation.1763 | loop fusion | bytes 524288 | tf_op jit(solution)/shard_map/slice | solution.py:43
  190.6 9.3 %reduce.2 = f32[2048,32]{1,0:T(8,128)S(1)} reduce(f32[2048,1,32]{2,1,0:T(1,128)S(1)} %bitcast.4716, f32[]{:T(128)} %broadcast.2033), dimensions={1}, to_apply=%bitcast.4050.reduce_sub_computation | reduce | bytes 524292
  200.4 11.8 %all_to_all.24 = f32[16,1,4096]{2,1,0:T(1,128)S(1)} all-to-all(f32[16,1,4096]{2,1,0:T(1,128)S(1)} %reshape.3600), channel_id=1, replica_groups=mesh['pl'=16,'xs'=16] {'pl'}, dimensions={0} | all-to-all | bytes 524288 | tf_op jit(solution)/shard_map/all_to_all | solution.py:90
  213.4 1.8 reshape.3601
  (894 shorter events, 63.7 us)
Async XLA Ops:
  2.3 8.4 %copy-start.113 = (f32[32,16,128]{2,1,0:T(8,128)S(1)}, f32[32,16,128]{2,1,0:T(8,128)}, u32[]{:S(2)}) copy-start(f32[32,16,128]{2,1,0:T(8,128)} %param.6) | copy-start | bytes 786436
  3.7 23.9 %all-to-all-start = ((f32[32,16,128]{2,0,1:T(8,128)}), f32[32,16,128]{2,0,1:T(8,128)S(1)}, u32[]{:S(2)}, u32[]{:S(2)}) async-start(f32[32,16,128]{2,0,1:T(8,128)} %bitcast.68), calls=%async_computation | async-start | bytes 524288 | tf_op jit(solution)/shard_map/all_to_all | solution.py:86
  13.6 12.6 %copy-start.112 = (f32[32,16,128]{2,1,0:T(8,128)S(1)}, f32[32,16,128]{2,1,0:T(8,128)}, u32[]{:S(2)}) copy-start(f32[32,16,128]{2,1,0:T(8,128)} %param.7) | copy-start | bytes 786436
  27.6 16.1 %all-to-all-start.1 = ((f32[32,16,128]{2,0,1:T(8,128)}), f32[32,16,128]{2,0,1:T(8,128)S(1)}, u32[]{:S(2)}, u32[]{:S(2)}) async-start(f32[32,16,128]{2,0,1:T(8,128)} %copy.1550), calls=%async_computation.1 | async-start | bytes 524288 | tf_op jit(solution)/shard_map/all_to_all | solution.py:257
  52.8 8.1 %copy-start.2 = (f32[32,1,512,1]{0,3,2,1:T(1,128)}, f32[32,1,512,1]{0,3,2,1:T(1,128)S(1)}, u32[]{:S(2)}) copy-start(f32[32,1,512,1]{0,3,2,1:T(1,128)S(1)} %get-tuple-element.347) | copy-start | bytes 196612
  53.3 7.6 %copy-start.4 = (f32[32,1,512,1]{0,3,2,1:T(1,128)}, f32[32,1,512,1]{0,3,2,1:T(1,128)S(1)}, u32[]{:S(2)}) copy-start(f32[32,1,512,1]{0,3,2,1:T(1,128)S(1)} %get-tuple-element.343) | copy-start | bytes 196612
  54.6 5.9 %copy-start.16 = (f32[32,1,256,1]{0,3,2,1:T(1,128)}, f32[32,1,256,1]{0,3,2,1:T(1,128)S(1)}, u32[]{:S(2)}) copy-start(f32[32,1,256,1]{0,3,2,1:T(1,128)S(1)} %get-tuple-element.372) | copy-start | bytes 98308
  54.8 5.7 %copy-start.18 = (f32[32,1,256,1]{0,3,2,1:T(1,128)}, f32[32,1,256,1]{0,3,2,1:T(1,128)S(1)}, u32[]{:S(2)}) copy-start(f32[32,1,256,1]{0,3,2,1:T(1,128)S(1)} %get-tuple-element.368) | copy-start | bytes 98308
  55.3 5.0 %copy-start.14 = (f32[32,1,128,1]{0,3,2,1:T(1,128)}, f32[32,1,128,1]{0,3,2,1:T(1,128)S(1)}, u32[]{:S(2)}) copy-start(f32[32,1,128,1]{0,3,2,1:T(1,128)S(1)} %get-tuple-element.399) | copy-start | bytes 49156
  55.7 4.6 %copy-start.41 = (f32[32,1,128,1]{0,3,2,1:T(1,128)}, f32[32,1,128,1]{0,3,2,1:T(1,128)S(1)}, u32[]{:S(2)}) copy-start(f32[32,1,128,1]{0,3,2,1:T(1,128)S(1)} %get-tuple-element.400) | copy-start | bytes 49156
  55.8 4.5 %copy-start.43 = (f32[32,1,128,1]{0,3,2,1:T(1,128)}, f32[32,1,128,1]{0,3,2,1:T(1,128)S(1)}, u32[]{:S(2)}) copy-start(f32[32,1,128,1]{0,3,2,1:T(1,128)S(1)} %get-tuple-element.396) | copy-start | bytes 49156
  56.1 4.0 %copy-start.35 = (f32[32,1,64,1]{0,3,2,1:T(1,128)}, f32[32,1,64,1]{0,3,2,1:T(1,128)S(1)}, u32[]{:S(2)}) copy-start(f32[32,1,64,1]{0,3,2,1:T(1,128)S(1)} %get-tuple-element.417) | copy-start | bytes 24580
  56.6 3.6 %copy-start.67 = (f32[32,1,64,1]{0,3,2,1:T(1,128)}, f32[32,1,64,1]{0,3,2,1:T(1,128)S(1)}, u32[]{:S(2)}) copy-start(f32[32,1,64,1]{0,3,2,1:T(1,128)S(1)} %get-tuple-element.418) | copy-start | bytes 24580
  56.6 3.6 %copy-start.71 = (f32[32,1,64,1]{0,3,2,1:T(1,128)}, f32[32,1,64,1]{0,3,2,1:T(1,128)S(1)}, u32[]{:S(2)}) copy-start(f32[32,1,64,1]{0,3,2,1:T(1,128)S(1)} %get-tuple-element.419) | copy-start | bytes 24580
  56.7 3.7 %copy-start.69 = (f32[32,1,64,1]{0,3,2,1:T(1,128)}, f32[32,1,64,1]{0,3,2,1:T(1,128)S(1)}, u32[]{:S(2)}) copy-start(f32[32,1,64,1]{0,3,2,1:T(1,128)S(1)} %get-tuple-element.414) | copy-start | bytes 24580
  56.7 3.7 %copy-start.100 = (f32[32,1,64]{0,2,1:T(8,128)}, f32[32,1,64]{0,2,1:T(8,128)S(1)}, u32[]{:S(2)}) copy-start(f32[32,1,64]{0,2,1:T(8,128)S(1)} %get-tuple-element.236) | copy-start | bytes 24580
  56.9 3.2 %copy-start.88 = (f32[32,1,32,1]{0,3,2,1:T(1,128)}, f32[32,1,32,1]{0,3,2,1:T(1,128)S(1)}, u32[]{:S(2)}) copy-start(f32[32,1,32,1]{0,3,2,1:T(1,128)S(1)} %get-tuple-element.434) | copy-start | bytes 12292
  64.2 18.8 %copy-start.60 = (f32[16,1,1,16,128]{4,1,0,3,2:T(1,128)S(1)}, f32[16,1,1,16,128]{4,1,0,3,2:T(1,128)}, u32[]{:S(2)}) copy-start(f32[16,1,1,16,128]{4,1,0,3,2:T(1,128)} %copy-done.59) | copy-start | bytes 393220
  64.2 19.5 %copy-start.64 = (f32[32,16,128]{2,0,1:T(8,128)S(1)}, f32[32,16,128]{2,0,1:T(8,128)}, u32[]{:S(2)}) copy-start(f32[32,16,128]{2,0,1:T(8,128)} %get-tuple-element.364) | copy-start | bytes 786436
  78.2 12.9 %all-to-all-start.2 = ((f32[16,1,4096]{2,1,0:T(1,128)}), f32[16,1,4096]{2,1,0:T(1,128)}, u32[]{:S(2)}, u32[]{:S(2)}) async-start(f32[16,1,4096]{2,1,0:T(1,128)} %reshape.3598), calls=%async_computation.2 | async-start | bytes 524288 | tf_op jit(solution)/shard_map/all_to_all | solution.py:90
  83.9 17.2 %copy-start.30 = (f32[32,16,128]{2,1,0:T(8,128)}, f32[32,16,128]{2,1,0:T(8,128)S(1)}, u32[]{:S(2)}) copy-start(f32[32,16,128]{2,1,0:T(8,128)S(1)} %copy.1633) | copy-start | bytes 786436
  85.1 17.0 %copy-start.32 = (f32[32,16,128]{2,1,0:T(8,128)}, f32[32,16,128]{2,1,0:T(8,128)S(1)}, u32[]{:S(2)}) copy-start(f32[32,16,128]{2,1,0:T(8,128)S(1)} %copy.1632) | copy-start | bytes 786436
  104.7 20.8 %copy-start = (f32[14,16,16,128]{3,2,1,0:T(8,128)S(1)}, f32[14,16,16,128]{3,2,1,0:T(8,128)}, u32[]{:S(2)}) copy-start(f32[14,16,16,128]{3,2,1,0:T(8,128)} %constant_dynamic-update-slice_fusion.13) | copy-start | bytes 5505028
  138.7 18.9 %copy-start.1 = (f32[14,16,16,128]{3,2,1,0:T(8,128)S(1)}, f32[14,16,16,128]{3,2,1,0:T(8,128)}, u32[]{:S(2)}) copy-start(f32[14,16,16,128]{3,2,1,0:T(8,128)} %constant_dynamic-update-slice_fusion.69) | copy-start | bytes 5505028
  (161 other events, 198.9 us)
where the time goes:
time: 223 us; the launch traced here: 219 us
  other arithmetic  63.6 us (29%)
  blocking collectives  63.3 us (28%)
  local copies, waits for them, and re-layouts  57.4 us (26%)
  starting transfers between devices  18.6 us (8%)
  waiting for transfers between devices  10 us (4%)
  between operations  6 us (3%)
    all_gather x2, blocking collectives, coupled(): gathered = lax.all_gather(boundary[None], 'xs', axis=0, tiled=True)  39.2 us
    unnamed x80, other arithmetic  26.3 us
    unnamed x406, local copies, waits for them, and re-layouts  21.7 us
    all_to_all x1, blocking collectives, to_lines(): return lax.all_to_all(values, 'pl', split_axis=1, concat_axis=2, tiled=True)  12.3 us
    all_to_all x1, blocking collectives, to_planes(): return lax.all_to_all(values, 'pl', split_axis=2, concat_axis=1, tiled=True)  11.8 us
    add x2, other arithmetic, matrix_vector(): matrix[2] * vector[0] + matrix[3] * vector[1]  10.1 us
    slice x42, local copies, waits for them, and re-layouts, halves(): return (paired[..., 0], paired[..., 1])  9.86 us
    all_to_all x1, starting transfers between devices, shards(): lax.all_to_all(northward_rate, 'pl', split_axis=1, concat_axis=2, tiled=T...  7.38 us
  transfers between devices with their start and end apart: 3, of which 2 were waited for; matrix products, arithmetic and copies ran while one was open for 11% of the time, Pallas kernels for 0%

commit v1 on v0

v1 whole, which is shorter than its diff:
```python
import functools

import jax
import jax.numpy as jnp
from jax import lax
from jax.experimental import pallas as pl
from jax.experimental.pallas import tpu as pltpu
from jax.sharding import PartitionSpec as P

MESH = pl.DeviceIdType.MESH
LANES = 128
HIGHEST = lax.Precision.HIGHEST


def reduced_factors(count, load, store):
    one = None
    b = None
    forward = []
    for j in range(count):
        left, right, shared = load(j)
        if b is None:
            b = jnp.zeros_like(left)
            one = jnp.ones_like(left)
        store("b", j, b)
        a1 = shared / (one - left * b)
        a2 = a1 * b
        store("a1", j, a1)
        store("a2", j, a2)
        b = right + a2 * shared
        forward.append(b)
    store("b", count, b)
    d = jnp.zeros_like(b)
    store("d", count, d)
    store("g", count, one)
    for j in reversed(range(count)):
        left, right, shared = load(j)
        c1 = shared / (one - right * d)
        c2 = c1 * d
        store("c1", j, c1)
        store("c2", j, c2)
        d = left + c2 * shared
        store("d", j, d)
        before = forward[j - 1] if j else jnp.zeros_like(d)
        store("g", j, one / (one - before * d))


def running(count, first, second, value, phi, psi, keep, emit):
    total = None
    for i in reversed(range(count)):
        term = second(i) * value(i)
        if total is None:
            total = jnp.zeros_like(term)
        keep(i, total)
        total = total + term
    total = jnp.zeros_like(total)
    for i in range(count):
        total = total + first(i) * value(i)
        emit(i, psi(i) * total + phi(i) * keep(i))


def kernel(
    nx, nz, n_pl, n_xs,
    source_hbm, vertical_hbm, north_hbm, east_hbm, out_ref,
    source, vertical, north, east,
    z_phi, z_psi, z_first, z_second,
    y_rate, y_phi, y_psi, y_first, y_second, y_value, y_part,
    x_phi, x_psi, x_phi2, x_psi2, x_first, x_second, x_first2, x_second2,
    x_part, x_part2, plane, hold,
    y_coef, y_ends, y_ends2, x_coef, x_coef_in, x_ends, x_ends_in, x_back, x_back_in,
    y_fac, y_scan, x_fac,
    load_sem, send_sem, recv_sem,
):
    lines = nx * nz
    blocks = lines // LANES
    pl_me, xs_me = lax.axis_index("pl"), lax.axis_index("xs")

    loads = []
    for slot, (hbm, vmem) in enumerate(
        ((north_hbm, north), (vertical_hbm, vertical), (source_hbm, source), (east_hbm, east))
    ):
        copy = pltpu.make_async_copy(hbm, vmem, load_sem.at[slot])
        copy.start()
        loads.append(copy)

    barrier = pltpu.get_barrier_semaphore()
    for o in range(1, n_pl):
        pl.semaphore_signal(barrier, 1, device_id={"pl": lax.rem(pl_me + o, n_pl)}, device_id_type=MESH)
    for o in range(1, n_xs):
        pl.semaphore_signal(barrier, 1, device_id={"xs": lax.rem(xs_me + o, n_xs)}, device_id_type=MESH)

    def share(axis, slot, pick, landing):
        count, me = (n_pl, pl_me) if axis == "pl" else (n_xs, xs_me)
        for o in range(1, count):
            peer = lax.rem(me + o, count)
            pltpu.make_async_remote_copy(
                src_ref=pick(peer),
                dst_ref=landing.at[me],
                send_sem=send_sem.at[slot],
                recv_sem=recv_sem.at[slot],
                device_id={axis: peer},
                device_id_type=MESH,
            ).start()

    def arrived(slot, landing, sem=None):
        count = landing.shape[0]
        if count > 1:
            whole = landing.at[pl.ds(0, count - 1)]
            sem = recv_sem if sem is None else sem
            pltpu.make_async_copy(whole, whole, sem.at[slot]).wait()

    def rows(b):
        return pl.ds(b * LANES, LANES)

    def across(y):
        return pl.ds(y, blocks, stride=LANES)

    loads[0].wait()
    for b in range(blocks):
        y_rate[rows(b)] = (1.0 / north[rows(b)]).T

    def y_sweep(i, carry):
        phi, phi_step, psi, psi_step = carry
        y_phi[across(i)] = phi
        y_psi[across(LANES - 1 - i)] = psi
        phi_step = phi_step + phi * y_rate[across(i)]
        psi_step = psi_step + psi * y_rate[across(LANES - 1 - i)]
        return phi + phi_step, phi_step, psi + psi_step, psi_step

    unit = jnp.ones((blocks, LANES), jnp.float32)
    y_phi_end = lax.fori_loop(0, LANES, y_sweep, (unit, unit, unit, unit), unroll=8)[0]
    y_inv = 1.0 / y_phi_end
    hold[pl.ds(0, blocks)] = y_inv
    for b in range(blocks):
        inv = hold[b:b + 1]
        scaled = y_rate[rows(b)] * inv
        y_first[rows(b)] = y_phi[rows(b)] * scaled
        y_second[rows(b)] = y_psi[rows(b)] * scaled
    y_coef[pl_me, 0] = y_psi[across(0)] * y_inv
    y_coef[pl_me, 1] = y_phi[across(LANES - 1)] * y_inv
    y_coef[pl_me, 2] = y_inv

    pl.semaphore_wait(barrier, n_pl + n_xs - 2)
    share("pl", 0, lambda peer: y_coef.at[pl_me], y_coef)

    def level(z):
        return pl.ds(z, nx, stride=nz)

    loads[1].wait()
    phi = jnp.ones((nx, LANES), jnp.float32)
    phi_step = psi = psi_step = phi
    for z in range(nz):
        back = nz - 1 - z
        up, down = 1.0 / vertical[level(z)], 1.0 / vertical[level(back)]
        z_phi[z] = phi
        z_psi[back] = psi
        z_first[z] = phi * up
        z_second[back] = psi * down
        phi_step = phi_step + phi * up
        psi_step = psi_step + psi * down
        phi = phi + phi_step
        psi = psi + psi_step
    z_inv = 1.0 / phi
    for z in range(nz):
        z_first[z] = z_first[z] * z_inv
        z_second[z] = z_second[z] * z_inv

    def z_solve(read, write):
        def keep(z, value=None):
            if value is None:
                return x_part2[pl.ds(z * nx, nx)]
            x_part2[pl.ds(z * nx, nx)] = value

        running(nz, lambda z: z_first[z], lambda z: z_second[z], read, lambda z: z_phi[z], lambda z: z_psi[z], keep, write)

    loads[2].wait()

    def to_plane(z, value):
        plane[level(z)] = value

    z_solve(lambda z: source[level(z)], to_plane)

    low = lax.broadcasted_iota(jnp.int32, (LANES, LANES), 0)
    high = lax.broadcasted_iota(jnp.int32, (LANES, LANES), 1)
    upto = jnp.where(high <= low, 1.0, 0.0)
    beyond = jnp.where(high > low, 1.0, 0.0)

    def y_send(slot, ends):
        for b in range(blocks):
            value = plane[rows(b)].T
            second = y_second[rows(b)] * value
            first = y_first[rows(b)] * value
            y_value[rows(b)] = first
            y_part[rows(b)] = second
            ends[pl_me, 0, b:b + 1] = jnp.sum(second, axis=0, keepdims=True)
            ends[pl_me, 1, b:b + 1] = jnp.sum(first, axis=0, keepdims=True)
        share("pl", slot, lambda peer: ends.at[pl_me], ends)

    def y_local():
        for b in range(blocks):
            below = jnp.dot(upto, y_value[rows(b)], precision=HIGHEST, preferred_element_type=jnp.float32)
            above = jnp.dot(beyond, y_part[rows(b)], precision=HIGHEST, preferred_element_type=jnp.float32)
            y_part[rows(b)] = y_psi[rows(b)] * below + y_phi[rows(b)] * above

    def y_finish(slot, ends):
        arrived(slot, ends)
        a = c = jnp.zeros((blocks, LANES), jnp.float32)
        y_scan[0, 0] = a
        y_scan[1, n_pl] = c
        for j in range(n_pl):
            k = n_pl - 1 - j
            a = ends[j, 1] + y_fac[2, j] * ends[j, 0] + y_fac[1, j] * a
            c = ends[k, 0] + y_fac[4, k] * ends[k, 1] + y_fac[3, k] * c
            y_scan[0, j + 1] = a
            y_scan[1, k] = c
        a_here, a_next = y_scan[0, pl_me], y_scan[0, pl_me + 1]
        c_here, c_next = y_scan[1, pl_me], y_scan[1, pl_me + 1]
        outside_low = (a_here + y_fac[0, pl_me] * c_here) * y_fac[6, pl_me]
        outside_high = (c_next + y_fac[5, pl_me + 1] * a_next) * y_fac[6, pl_me + 1]
        inv = y_coef[pl_me, 2]
        hold[pl.ds(0, blocks)] = outside_low * inv
        hold[pl.ds(blocks, blocks)] = outside_high * inv
        for b in range(blocks):
            solved = (
                y_part[rows(b)]
                + y_psi[rows(b)] * hold[b:b + 1]
                + y_phi[rows(b)] * hold[blocks + b:blocks + b + 1]
            )
            plane[rows(b)] = solved.T

    y_send(1, y_ends)

    def step(i):
        return pl.ds(i * nz, nz)

    loads[3].wait()
    phi = jnp.ones((nz, LANES), jnp.float32)
    phi_step = psi = psi_step = phi
    for i in range(nx):
        back = nx - 1 - i
        up, down = 1.0 / east[step(i)], 1.0 / east[step(back)]
        x_phi[step(i)] = phi
        x_psi[step(back)] = psi
        x_first[step(i)] = phi * up
        x_second[step(back)] = psi * down
        phi_step = phi_step + phi * up
        psi_step = psi_step + psi * down
        phi = phi + phi_step
        psi = psi + psi_step
    x_inv = 1.0 / phi
    for i in range(nx):
        x_first[step(i)] = x_first[step(i)] * x_inv
        x_second[step(i)] = x_second[step(i)] * x_inv

    def x_solve(read, write):
        def keep(i, value=None):
            if value is None:
                return x_part2[step(i)]
            x_part2[step(i)] = value

        running(
            nx, lambda i: x_first[step(i)], lambda i: x_second[step(i)], read,
            lambda i: x_phi[step(i)], lambda i: x_psi[step(i)], keep, write,
        )

    def into(ref):
        def write(i, value):
            ref[step(i)] = value

        return write

    x_solve(lambda i: x_phi[step(i)], into(x_phi2))
    x_solve(lambda i: x_psi[step(i)], into(x_psi2))
    for i in range(nx):
        scaled = x_inv * (1.0 / east[step(i)])
        x_first2[step(i)] = x_phi2[step(i)] * scaled
        x_second2[step(i)] = x_psi2[step(i)] * scaled
    last = step(nx - 1)
    x_coef[:, 0] = x_psi[step(0)] * x_inv
    x_coef[:, 1] = x_phi[last] * x_inv
    x_coef[:, 2] = x_inv
    x_coef[:, 3] = x_psi2[step(0)] * x_inv
    x_coef[:, 4] = x_phi2[last] * x_inv
    x_coef[:, 5] = x_phi2[step(0)] * x_inv
    x_coef[:, 6] = x_inv
    x_coef[:, 7] = x_inv
    share("xs", 2, lambda peer: x_coef.at[peer], x_coef_in)
    x_coef_in[xs_me] = x_coef[xs_me]

    names = {"b": 0, "a1": 1, "a2": 2, "c1": 3, "c2": 4, "d": 5, "g": 6}
    arrived(0, y_coef)

    def y_store(name, j, value):
        y_fac[names[name], j] = value

    reduced_factors(n_pl, lambda j: (y_coef[j, 0], y_coef[j, 1], y_coef[j, 2]), y_store)
    y_local()
    y_finish(1, y_ends)

    p0 = pn = q0 = qn = jnp.zeros((nz, LANES), jnp.float32)
    for i in range(nx):
        value = plane[step(i)]
        p0 = p0 + x_second[step(i)] * value
        pn = pn + x_first[step(i)] * value
        q0 = q0 + x_second2[step(i)] * value
        qn = qn + x_first2[step(i)] * value
    x_ends[:, 0] = p0
    x_ends[:, 1] = pn
    x_ends[:, 2] = q0
    x_ends[:, 3] = qn
    share("xs", 3, lambda peer: x_ends.at[peer], x_ends_in)
    x_ends_in[xs_me] = x_ends[xs_me]

    arrived(2, x_coef_in)

    def x_store(name, j, value):
        x_fac[names[name], j:j + 1] = value

    reduced_factors(
        n_xs, lambda j: (x_coef_in[j, 0:1], x_coef_in[j, 1:2], x_coef_in[j, 2:3]), x_store
    )
    x_solve(lambda i: plane[step(i)], into(x_part))

    arrived(3, x_ends_in)

    def fac(name, j):
        return x_fac[names[name], j:j + 1]

    def x_reduced(ends):
        a = c = jnp.zeros((1, LANES), jnp.float32)
        lefts, rights = [a], [c]
        for j in range(n_xs):
            k = n_xs - 1 - j
            a = ends[j][1] + fac("a2", j) * ends[j][0] + fac("a1", j) * a
            c = ends[k][0] + fac("c2", k) * ends[k][1] + fac("c1", k) * c
            lefts.append(a)
            rights.append(c)
        rights = rights[::-1]
        lows = [(lefts[j] + fac("b", j) * rights[j]) * fac("g", j) for j in range(n_xs)]
        highs = [
            (rights[j + 1] + fac("d", j + 1) * lefts[j + 1]) * fac("g", j + 1) for j in range(n_xs)
        ]
        return lows, highs

    lows, highs = x_reduced([(x_ends_in[j, 0:1], x_ends_in[j, 1:2]) for j in range(n_xs)])
    again = []
    for j in range(n_xs):
        left, right, shared = x_coef_in[j, 3:4], x_coef_in[j, 4:5], x_coef_in[j, 5:6]
        again.append(
            (
                x_ends_in[j, 2:3] + left * lows[j] + shared * highs[j],
                x_ends_in[j, 3:4] + shared * lows[j] + right * highs[j],
            )
        )
    lows2, highs2 = x_reduced(again)
    for j in range(n_xs):
        inv = x_coef_in[j, 2:3]
        x_back[j, 0:1] = lows[j] * inv
        x_back[j, 1:2] = highs[j] * inv
        x_back[j, 2:3] = lows2[j] * inv
        x_back[j, 3:4] = highs2[j] * inv
    share("xs", 4, lambda peer: x_back.at[peer], x_back_in)
    x_back_in[xs_me] = x_back[xs_me]

    x_solve(lambda i: x_part[step(i)], into(x_part))
    arrived(4, x_back_in)
    low1, high1, low2, high2 = (x_back_in[:, q] for q in range(4))
    for i in range(nx):
        plane[step(i)] = (
            x_part[step(i)]
            + x_psi2[step(i)] * low1
            + x_phi2[step(i)] * high1
            + x_psi[step(i)] * low2
            + x_phi[step(i)] * high2
        )

    y_send(5, y_ends2)
    y_local()
    y_finish(5, y_ends2)

    def to_out(z, value):
        out_ref[level(z)] = value

    z_solve(lambda z: plane[level(z)], to_out)

    arrived(0, y_coef, send_sem)
    arrived(1, y_ends, send_sem)
    arrived(2, x_coef_in, send_sem)
    arrived(3, x_ends_in, send_sem)
    arrived(4, x_back_in, send_sem)
    arrived(5, y_ends2, send_sem)


def shards(n_pl, n_xs, source, eastward_rate, northward_rate, vertical_rate, amplitude):
    nx, nz, ny = source.shape
    lines = nx * nz
    blocks = lines // LANES
    flat = lambda array: array.reshape(lines, ny)
    field = pltpu.VMEM((lines, LANES), jnp.float32)
    column = pltpu.VMEM((nz, nx, LANES), jnp.float32)
    vmem = lambda *shape: pltpu.VMEM(shape, jnp.float32)
    second = pl.pallas_call(
        functools.partial(kernel, nx, nz, n_pl, n_xs),
        out_shape=jax.ShapeDtypeStruct((lines, ny), jnp.float32),
        in_specs=[pl.BlockSpec(memory_space=pl.ANY)] * 4,
        out_specs=pl.BlockSpec(memory_space=pltpu.VMEM),
        scratch_shapes=[field] * 4
        + [column] * 4
        + [field] * 7
        + [field] * 8
        + [field] * 3
        + [vmem(2 * blocks, LANES)]
        + [
            vmem(n_pl, 3, blocks, LANES),
            vmem(n_pl, 2, blocks, LANES),
            vmem(n_pl, 2, blocks, LANES),
            vmem(n_xs, 8, LANES),
            vmem(n_xs, 8, LANES),
            vmem(n_xs, 4, LANES),
            vmem(n_xs, 4, LANES),
            vmem(n_xs, 4, LANES),
            vmem(n_xs, 4, LANES),
            vmem(7, n_pl + 1, blocks, LANES),
            vmem(2, n_pl + 1, blocks, LANES),
            vmem(7, n_xs + 1, LANES),
            pltpu.SemaphoreType.DMA((4,)),
            pltpu.SemaphoreType.DMA((6,)),
            pltpu.SemaphoreType.DMA((6,)),
        ],
        compiler_params=pltpu.CompilerParams(
            collective_id=0, has_side_effects=True, vmem_limit_bytes=40 * 1024 * 1024
        ),
        name="adi",
    )(flat(source), flat(vertical_rate), flat(northward_rate), flat(eastward_rate))
    return amplitude * second.reshape(nx, nz, ny)


def solution(mesh):
    spec = P("xs", None, "pl")
    return jax.shard_map(
        functools.partial(shards, mesh.shape["pl"], mesh.shape["xs"]),
        mesh=mesh,
        in_specs=(spec,) * 5,
        out_specs=spec,
        check_vma=False,
    )
```

time: 223 us -> 35.1 us (0.16)
  the two profiles are of different devices: /device:TPU:32 before, /device:TPU:1 now
where the time goes in v1:
time: 35.1 us; the launch traced here: 34.9 us
  Pallas kernels  30.3 us (86%)
  local copies, waits for them, and re-layouts  3.8 us (11%)
  other arithmetic  0.74 us (2%)
    pallas_call x1, Pallas kernels, shards(): pl.pallas_call(functools.partial(kernel, nx, nz, n_pl, n_xs), out_shape=j...  30.3 us
    unnamed x10, local copies, waits for them, and re-layouts  3.8 us
    mul x1, other arithmetic, shards(): return amplitude * second.reshape(nx, nz, ny)  0.74 us

profile of v1, /device:TPU:1, one launch (start us, length us, event | category | flops | bytes accessed | tf_op | source)
XLA Modules:
  0.0 34.9 jit_solution(1123557086860410336)
XLA Ops:
  0.0 0.0 copy-start
  0.0 0.9 %copy-done = f32[32,16,128]{2,1,0:T(8,128)S(1)} copy-done((f32[32,16,128]{2,1,0:T(8,128)S(1)}, f32[32,16,128]{2,1,0:T(8,128)}, u32[]{:S(2)}) %copy-start) | copy-done | bytes 262168
  1.0 0.0 copy-start.1
  1.0 0.9 %copy-done.1 = f32[32,16,128]{2,1,0:T(8,128)S(1)} copy-done((f32[32,16,128]{2,1,0:T(8,128)S(1)}, f32[32,16,128]{2,1,0:T(8,128)}, u32[]{:S(2)}) %copy-start.1) | copy-done | bytes 262168
  1.9 0.0 copy-start.2
  1.9 0.9 %copy-done.2 = f32[32,16,128]{2,1,0:T(8,128)S(1)} copy-done((f32[32,16,128]{2,1,0:T(8,128)S(1)}, f32[32,16,128]{2,1,0:T(8,128)}, u32[]{:S(2)}) %copy-start.2) | copy-done | bytes 262168
  2.9 0.0 copy-start.3
  2.9 0.9 %copy-done.3 = f32[32,16,128]{2,1,0:T(8,128)S(1)} copy-done((f32[32,16,128]{2,1,0:T(8,128)S(1)}, f32[32,16,128]{2,1,0:T(8,128)}, u32[]{:S(2)}) %copy-start.3) | copy-done | bytes 262168
  3.8 0.0 copy-start.4
  3.8 30.3 %adi.1 = f32[512,128]{1,0:T(8,128)S(1)} custom-call(f32[512,128]{1,0:T(8,128)S(1)} %bitcast.6, f32[512,128]{1,0:T(8,128)S(1)} %bitcast.7, f32[512,128]{1,0:T(8,128)S(1)} %bitcast.8, f32[512,128]{1,0:T(8,128)S(1)} %bitcast.9), custom_call_target="tpu_custom_call" | custom-call | tf_op jit(solution)/shard_map/adi/pallas_call | solution.py:401
  34.1 0.0 copy-done.4
  34.2 0.7 %mul.3 = f32[32,16,128]{2,1,0:T(8,128)} multiply(f32[32,16,128]{2,1,0:T(8,128)S(1)} %copy-done.4, f32[32,16,128]{2,1,0:T(8,128)S(1)} %bitcast.5) | non-fusion elementwise | flops 65536 | bytes 786432 | tf_op jit(solution)/shard_map/mul | solution.py:434
Async XLA Ops:
  0.0 0.9 %copy-start = (f32[32,16,128]{2,1,0:T(8,128)S(1)}, f32[32,16,128]{2,1,0:T(8,128)}, u32[]{:S(2)}) copy-start(f32[32,16,128]{2,1,0:T(8,128)} %param.5) | copy-start | bytes 786436
  1.0 0.9 %copy-start.1 = (f32[32,16,128]{2,1,0:T(8,128)S(1)}, f32[32,16,128]{2,1,0:T(8,128)}, u32[]{:S(2)}) copy-start(f32[32,16,128]{2,1,0:T(8,128)} %param.8) | copy-start | bytes 786436
  1.9 0.9 %copy-start.2 = (f32[32,16,128]{2,1,0:T(8,128)S(1)}, f32[32,16,128]{2,1,0:T(8,128)}, u32[]{:S(2)}) copy-start(f32[32,16,128]{2,1,0:T(8,128)} %param.7) | copy-start | bytes 786436
  2.9 0.9 %copy-start.3 = (f32[32,16,128]{2,1,0:T(8,128)S(1)}, f32[32,16,128]{2,1,0:T(8,128)}, u32[]{:S(2)}) copy-start(f32[32,16,128]{2,1,0:T(8,128)} %param.6) | copy-start | bytes 786436
  3.8 30.3 %copy-start.4 = (f32[32,16,128]{2,1,0:T(8,128)S(1)}, f32[32,16,128]{2,1,0:T(8,128)}, u32[]{:S(2)}) copy-start(f32[32,16,128]{2,1,0:T(8,128)} %param.9) | copy-start | bytes 786436

commit v2 on v1

--- a/solution.py
+++ b/solution.py
@@ -1,4 +1,5 @@
 import functools
+import math
 
 import jax
 import jax.numpy as jnp
@@ -74,6 +75,28 @@
     blocks = lines // LANES
     pl_me, xs_me = lax.axis_index("pl"), lax.axis_index("xs")
 
+    side, chips, half = math.isqrt(n_pl), n_xs // 2, n_xs // 2
+    pl_row, pl_col = pl_me // side, lax.rem(pl_me, side)
+    chip, core = xs_me // 2, lax.rem(xs_me, 2)
+    pair = lax.rem(xs_me, half)
+
+    def ring(offset, count):
+        return min(offset, count - offset)
+
+    steps = [(r, c) for r in range(side) for c in range(side) if r or c]
+    steps.sort(key=lambda step: -ring(step[0], side) - ring(step[1], side))
+    pl_peers = [lax.rem(pl_row + r, side) * side + lax.rem(pl_col + c, side) for r, c in steps]
+    xs_offsets = sorted(range(1, n_xs), key=lambda offset: -ring(offset, n_xs))
+    xs_peers = [lax.rem(xs_me + offset, n_xs) for offset in xs_offsets]
+    near = sorted(range(-(chips // 8), chips // 2 - chips // 8), key=lambda offset: -abs(offset))
+    near_peers = [lax.rem(chip + offset + chips, chips) * 2 + c for offset in near if offset for c in range(2)]
+    near_peers.append(xs_me + 1 - 2 * core)
+
+    barrier = pltpu.get_barrier_semaphore()
+    for axis, peers in (("xs", xs_peers), ("pl", pl_peers)):
+        for peer in peers:
+            pl.semaphore_signal(barrier, 1, device_id={axis: peer}, device_id_type=MESH)
+
     loads = []
     for slot, (hbm, vmem) in enumerate(
         ((north_hbm, north), (vertical_hbm, vertical), (source_hbm, source), (east_hbm, east))
@@ -82,19 +105,11 @@
         copy.start()
         loads.append(copy)
 
-    barrier = pltpu.get_barrier_semaphore()
-    for o in range(1, n_pl):
-        pl.semaphore_signal(barrier, 1, device_id={"pl": lax.rem(pl_me + o, n_pl)}, device_id_type=MESH)
-    for o in range(1, n_xs):
-        pl.semaphore_signal(barrier, 1, device_id={"xs": lax.rem(xs_me + o, n_xs)}, device_id_type=MESH)
-
-    def share(axis, slot, pick, landing):
-        count, me = (n_pl, pl_me) if axis == "pl" else (n_xs, xs_me)
-        for o in range(1, count):
-            peer = lax.rem(me + o, count)
+    def share(axis, slot, peers, pick, landing, place):
+        for peer in peers:
             pltpu.make_async_remote_copy(
                 src_ref=pick(peer),
-                dst_ref=landing.at[me],
+                dst_ref=landing.at[place],
                 send_sem=send_sem.at[slot],
                 recv_sem=recv_sem.at[slot],
                 device_id={axis: peer},
@@ -140,7 +155,7 @@
     y_coef[pl_me, 2] = y_inv
 
     pl.semaphore_wait(barrier, n_pl + n_xs - 2)
-    share("pl", 0, lambda peer: y_coef.at[pl_me], y_coef)
+    share("pl", 0, pl_peers, lambda peer: y_coef.at[pl_me], y_coef, pl_me)
 
     def level(z):
         return pl.ds(z, nx, stride=nz)
@@ -193,7 +208,7 @@
             y_part[rows(b)] = second
             ends[pl_me, 0, b:b + 1] = jnp.sum(second, axis=0, keepdims=True)
             ends[pl_me, 1, b:b + 1] = jnp.sum(first, axis=0, keepdims=True)
-        share("pl", slot, lambda peer: ends.at[pl_me], ends)
+        share("pl", slot, pl_peers, lambda peer: ends.at[pl_me], ends, pl_me)
 
     def y_local():
         for b in range(blocks):
@@ -275,16 +290,18 @@
         x_first2[step(i)] = x_phi2[step(i)] * scaled
         x_second2[step(i)] = x_psi2[step(i)] * scaled
     last = step(nx - 1)
-    x_coef[:, 0] = x_psi[step(0)] * x_inv
-    x_coef[:, 1] = x_phi[last] * x_inv
-    x_coef[:, 2] = x_inv
-    x_coef[:, 3] = x_psi2[step(0)] * x_inv
-    x_coef[:, 4] = x_phi2[last] * x_inv
-    x_coef[:, 5] = x_phi2[step(0)] * x_inv
-    x_coef[:, 6] = x_inv
-    x_coef[:, 7] = x_inv
-    share("xs", 2, lambda peer: x_coef.at[peer], x_coef_in)
-    x_coef_in[xs_me] = x_coef[xs_me]
+    def halves(ref, quantity, value):
+        group, at = quantity
+        for k in range(2):
+            ref[(slice(None),) + group + (at + k,)] = value[k * half:(k + 1) * half]
+
+    coefficients = (
+        x_psi[step(0)], x_phi[last], None, x_psi2[step(0)], x_phi2[last], x_phi2[step(0)],
+    )
+    for q, value in enumerate(coefficients):
+        halves(x_coef, ((q // 2,), q % 2 * 2), x_inv if value is None else value * x_inv)
+    share("xs", 2, xs_peers, lambda peer: x_coef.at[lax.rem(peer, half)], x_coef_in, xs_me)
+    x_coef_in[xs_me] = x_coef[pair]
 
     names = {"b": 0, "a1": 1, "a2": 2, "c1": 3, "c2": 4, "d": 5, "g": 6}
     arrived(0, y_coef)
@@ -303,30 +320,29 @@
         pn = pn + x_first[step(i)] * value
         q0 = q0 + x_second2[step(i)] * value
         qn = qn + x_first2[step(i)] * value
-    x_ends[:, 0] = p0
-    x_ends[:, 1] = pn
-    x_ends[:, 2] = q0
-    x_ends[:, 3] = qn
-    share("xs", 3, lambda peer: x_ends.at[peer], x_ends_in)
-    x_ends_in[xs_me] = x_ends[xs_me]
+    for q, value in enumerate((p0, pn, q0, qn)):
+        halves(x_ends, ((), 2 * q), value)
+    share("xs", 3, xs_peers, lambda peer: x_ends.at[lax.rem(peer, half)], x_ends_in, xs_me)
+    x_ends_in[xs_me] = x_ends[pair]
 
     arrived(2, x_coef_in)
 
     def x_store(name, j, value):
-        x_fac[names[name], j:j + 1] = value
-
-    reduced_factors(
-        n_xs, lambda j: (x_coef_in[j, 0:1], x_coef_in[j, 1:2], x_coef_in[j, 2:3]), x_store
-    )
+        x_fac[names[name], j] = value
+
+    def coef(j, q):
+        return x_coef_in[j, q // 2, q % 2 * 2:q % 2 * 2 + 2]
+
+    reduced_factors(n_xs, lambda j: (coef(j, 0), coef(j, 1), coef(j, 2)), x_store)
     x_solve(lambda i: plane[step(i)], into(x_part))
 
     arrived(3, x_ends_in)
 
     def fac(name, j):
-        return x_fac[names[name], j:j + 1]
+        return x_fac[names[name], j]
 
     def x_reduced(ends):
-        a = c = jnp.zeros((1, LANES), jnp.float32)
+        a = c = jnp.zeros((2, LANES), jnp.float32)
         lefts, rights = [a], [c]
         for j in range(n_xs):
             k = n_xs - 1 - j
@@ -341,29 +357,31 @@
         ]
         return lows, highs
 
-    lows, highs = x_reduced([(x_ends_in[j, 0:1], x_ends_in[j, 1:2]) for j in range(n_xs)])
+    def end(j, q):
+        return x_ends_in[j, 2 * q:2 * q + 2]
+
+    lows, highs = x_reduced([(end(j, 0), end(j, 1)) for j in range(n_xs)])
     again = []
     for j in range(n_xs):
-        left, right, shared = x_coef_in[j, 3:4], x_coef_in[j, 4:5], x_coef_in[j, 5:6]
+        left, right, shared = coef(j, 3), coef(j, 4), coef(j, 5)
         again.append(
             (
-                x_ends_in[j, 2:3] + left * lows[j] + shared * highs[j],
-                x_ends_in[j, 3:4] + shared * lows[j] + right * highs[j],
+                end(j, 2) + left * lows[j] + shared * highs[j],
+                end(j, 3) + shared * lows[j] + right * highs[j],
             )
         )
     lows2, highs2 = x_reduced(again)
     for j in range(n_xs):
-        inv = x_coef_in[j, 2:3]
-        x_back[j, 0:1] = lows[j] * inv
-        x_back[j, 1:2] = highs[j] * inv
-        x_back[j, 2:3] = lows2[j] * inv
-        x_back[j, 3:4] = highs2[j] * inv
-    share("xs", 4, lambda peer: x_back.at[peer], x_back_in)
-    x_back_in[xs_me] = x_back[xs_me]
+        for q, value in enumerate((lows[j], highs[j], lows2[j], highs2[j])):
+            x_back[j, 2 * q:2 * q + 2] = value * coef(j, 2)
+    share("xs", 4, near_peers, lambda peer: x_back.at[peer], x_back_in, pair)
+    x_back_in[pair] = x_back[xs_me]
 
     x_solve(lambda i: x_part[step(i)], into(x_part))
     arrived(4, x_back_in)
-    low1, high1, low2, high2 = (x_back_in[:, q] for q in range(4))
+    low1, high1, low2, high2 = (
+        jnp.concatenate([x_back_in[:, 2 * q], x_back_in[:, 2 * q + 1]], axis=0) for q in range(4)
+    )
     for i in range(nx):
         plane[step(i)] = (
             x_part[step(i)]
@@ -394,14 +412,14 @@
     nx, nz, ny = source.shape
     lines = nx * nz
     blocks = lines // LANES
-    flat = lambda array: array.reshape(lines, ny)
+    flat = lambda array: pltpu.with_memory_space_constraint(array.reshape(lines, ny), pltpu.HBM)
     field = pltpu.VMEM((lines, LANES), jnp.float32)
     column = pltpu.VMEM((nz, nx, LANES), jnp.float32)
     vmem = lambda *shape: pltpu.VMEM(shape, jnp.float32)
     second = pl.pallas_call(
         functools.partial(kernel, nx, nz, n_pl, n_xs),
         out_shape=jax.ShapeDtypeStruct((lines, ny), jnp.float32),
-        in_specs=[pl.BlockSpec(memory_space=pl.ANY)] * 4,
+        in_specs=[pl.BlockSpec(memory_space=pltpu.HBM)] * 4,
         out_specs=pl.BlockSpec(memory_space=pltpu.VMEM),
         scratch_shapes=[field] * 4
         + [column] * 4
@@ -413,15 +431,15 @@
             vmem(n_pl, 3, blocks, LANES),
             vmem(n_pl, 2, blocks, LANES),
             vmem(n_pl, 2, blocks, LANES),
+            vmem(n_xs // 2, 3, 4, LANES),
+            vmem(n_xs, 3, 4, LANES),
+            vmem(n_xs // 2, 8, LANES),
             vmem(n_xs, 8, LANES),
             vmem(n_xs, 8, LANES),
-            vmem(n_xs, 4, LANES),
-            vmem(n_xs, 4, LANES),
-            vmem(n_xs, 4, LANES),
-            vmem(n_xs, 4, LANES),
+            vmem(n_xs // 2, 8, LANES),
             vmem(7, n_pl + 1, blocks, LANES),
             vmem(2, n_pl + 1, blocks, LANES),
-            vmem(7, n_xs + 1, LANES),
+            vmem(7, n_xs + 1, 2, LANES),
             pltpu.SemaphoreType.DMA((4,)),
             pltpu.SemaphoreType.DMA((6,)),
             pltpu.SemaphoreType.DMA((6,)),

time: 35.1 us -> 29.7 us (0.85)
  local copies, waits for them, and re-layouts: 3.8 us -> 0.01 us
  Pallas kernels: 30.3 us -> 28.8 us
    unnamed x10 -> x2, local copies, waits for them, and re-layouts: 3.8 us -> 0.01 us
    pallas_call x1, Pallas kernels: 30.3 us -> 28.8 us  [shards(): pl.pallas_call(functools.partial(kernel, nx, nz, n_pl, n_xs), out_shape=j...]
where the time goes in v2:
time: 29.7 us; the launch traced here: 29.6 us
  Pallas kernels  28.8 us (97%)
  other arithmetic  0.74 us (2%)
    pallas_call x1, Pallas kernels, shards(): pl.pallas_call(functools.partial(kernel, nx, nz, n_pl, n_xs), out_shape=j...  28.8 us
    mul x1, other arithmetic, shards(): return amplitude * second.reshape(nx, nz, ny)  0.74 us

profile of v2, /device:TPU:1, one launch (start us, length us, event | category | flops | bytes accessed | tf_op | source)
XLA Modules:
  0.0 29.6 jit_solution(4802793306386437646)
XLA Ops:
  0.0 0.0 copy-start
  0.0 28.8 %adi.1 = f32[512,128]{1,0:T(8,128)S(1)} custom-call(f32[512,128]{1,0:T(8,128)} %bitcast.6, f32[512,128]{1,0:T(8,128)} %bitcast.7, f32[512,128]{1,0:T(8,128)} %bitcast.8, f32[512,128]{1,0:T(8,128)} %bitcast.9), custom_call_target="tpu_custom_call" | custom-call | tf_op jit(solution)/shard_map/adi/pallas_call | solution.py:419
  28.8 0.0 copy-done
  28.8 0.7 %mul.3 = f32[32,16,128]{2,1,0:T(8,128)} multiply(f32[32,16,128]{2,1,0:T(8,128)S(1)} %copy-done, f32[32,16,128]{2,1,0:T(8,128)S(1)} %bitcast.5) | non-fusion elementwise | flops 65536 | bytes 786432 | tf_op jit(solution)/shard_map/mul | solution.py:452
Async XLA Ops:
  0.0 28.8 %copy-start = (f32[32,16,128]{2,1,0:T(8,128)S(1)}, f32[32,16,128]{2,1,0:T(8,128)}, u32[]{:S(2)}) copy-start(f32[32,16,128]{2,1,0:T(8,128)} %param.9) | copy-start | bytes 786436

commit v3 on v2

--- a/solution.py
+++ b/solution.py
@@ -67,18 +67,18 @@
     y_rate, y_phi, y_psi, y_first, y_second, y_value, y_part,
     x_phi, x_psi, x_phi2, x_psi2, x_first, x_second, x_first2, x_second2,
     x_part, x_part2, plane, hold,
-    y_coef, y_ends, y_ends2, x_coef, x_coef_in, x_ends, x_ends_in, x_back, x_back_in,
-    y_fac, y_scan, x_fac,
+    y_coef, y_ends, y_ends2, x_coef, x_two_coef, x_chip_coef, x_ends, x_two, x_chip,
+    x_outside, x_back, x_back_in, x_meet, y_fac, y_scan, x_fac,
     load_sem, send_sem, recv_sem,
 ):
     lines = nx * nz
     blocks = lines // LANES
     pl_me, xs_me = lax.axis_index("pl"), lax.axis_index("xs")
 
-    side, chips, half = math.isqrt(n_pl), n_xs // 2, n_xs // 2
+    side, chips, half = math.isqrt(n_pl), n_xs // 2, nz // 2
     pl_row, pl_col = pl_me // side, lax.rem(pl_me, side)
     chip, core = xs_me // 2, lax.rem(xs_me, 2)
-    pair = lax.rem(xs_me, half)
+    other = 1 - core
 
     def ring(offset, count):
         return min(offset, count - offset)
@@ -86,14 +86,12 @@
     steps = [(r, c) for r in range(side) for c in range(side) if r or c]
     steps.sort(key=lambda step: -ring(step[0], side) - ring(step[1], side))
     pl_peers = [lax.rem(pl_row + r, side) * side + lax.rem(pl_col + c, side) for r, c in steps]
-    xs_offsets = sorted(range(1, n_xs), key=lambda offset: -ring(offset, n_xs))
-    xs_peers = [lax.rem(xs_me + offset, n_xs) for offset in xs_offsets]
-    near = sorted(range(-(chips // 8), chips // 2 - chips // 8), key=lambda offset: -abs(offset))
-    near_peers = [lax.rem(chip + offset + chips, chips) * 2 + c for offset in near if offset for c in range(2)]
-    near_peers.append(xs_me + 1 - 2 * core)
+    ring_offsets = sorted(range(1, chips), key=lambda offset: -ring(offset, chips))
+    ring_peers = [lax.rem(chip + offset, chips) * 2 + core for offset in ring_offsets]
+    mate = [chip * 2 + other]
 
     barrier = pltpu.get_barrier_semaphore()
-    for axis, peers in (("xs", xs_peers), ("pl", pl_peers)):
+    for axis, peers in (("pl", pl_peers), ("xs", ring_peers + mate)):
         for peer in peers:
             pl.semaphore_signal(barrier, 1, device_id={axis: peer}, device_id_type=MESH)
 
@@ -105,11 +103,11 @@
         copy.start()
         loads.append(copy)
 
-    def share(axis, slot, peers, pick, landing, place):
+    def share(axis, slot, peers, source_ref, landing_ref):
         for peer in peers:
             pltpu.make_async_remote_copy(
-                src_ref=pick(peer),
-                dst_ref=landing.at[place],
+                src_ref=source_ref,
+                dst_ref=landing_ref,
                 send_sem=send_sem.at[slot],
                 recv_sem=recv_sem.at[slot],
                 device_id={axis: peer},
@@ -117,11 +115,11 @@
             ).start()
 
     def arrived(slot, landing, sem=None):
-        count = landing.shape[0]
-        if count > 1:
-            whole = landing.at[pl.ds(0, count - 1)]
-            sem = recv_sem if sem is None else sem
-            pltpu.make_async_copy(whole, whole, sem.at[slot]).wait()
+        sem = recv_sem if sem is None else sem
+        pltpu.make_async_copy(landing, landing, sem.at[slot]).wait()
+
+    def others(landing):
+        return landing.at[pl.ds(0, landing.shape[0] - 1)]
 
     def rows(b):
         return pl.ds(b * LANES, LANES)
@@ -154,8 +152,8 @@
     y_coef[pl_me, 1] = y_phi[across(LANES - 1)] * y_inv
     y_coef[pl_me, 2] = y_inv
 
-    pl.semaphore_wait(barrier, n_pl + n_xs - 2)
-    share("pl", 0, pl_peers, lambda peer: y_coef.at[pl_me], y_coef, pl_me)
+    pl.semaphore_wait(barrier, n_pl + chips - 1)
+    share("pl", 0, pl_peers, y_coef.at[pl_me], y_coef.at[pl_me])
 
     def level(z):
         return pl.ds(z, nx, stride=nz)
@@ -208,7 +206,7 @@
             y_part[rows(b)] = second
             ends[pl_me, 0, b:b + 1] = jnp.sum(second, axis=0, keepdims=True)
             ends[pl_me, 1, b:b + 1] = jnp.sum(first, axis=0, keepdims=True)
-        share("pl", slot, pl_peers, lambda peer: ends.at[pl_me], ends, pl_me)
+        share("pl", slot, pl_peers, ends.at[pl_me], ends.at[pl_me])
 
     def y_local():
         for b in range(blocks):
@@ -217,7 +215,7 @@
             y_part[rows(b)] = y_psi[rows(b)] * below + y_phi[rows(b)] * above
 
     def y_finish(slot, ends):
-        arrived(slot, ends)
+        arrived(slot, others(ends))
         a = c = jnp.zeros((blocks, LANES), jnp.float32)
         y_scan[0, 0] = a
         y_scan[1, n_pl] = c
@@ -290,27 +288,57 @@
         x_first2[step(i)] = x_phi2[step(i)] * scaled
         x_second2[step(i)] = x_psi2[step(i)] * scaled
     last = step(nx - 1)
-    def halves(ref, quantity, value):
-        group, at = quantity
-        for k in range(2):
-            ref[(slice(None),) + group + (at + k,)] = value[k * half:(k + 1) * half]
-
     coefficients = (
-        x_psi[step(0)], x_phi[last], None, x_psi2[step(0)], x_phi2[last], x_phi2[step(0)],
+        x_psi[step(0)] * x_inv, x_phi[last] * x_inv, x_inv,
+        x_psi2[step(0)] * x_inv, x_phi2[last] * x_inv, x_phi2[step(0)] * x_inv,
     )
     for q, value in enumerate(coefficients):
-        halves(x_coef, ((q // 2,), q % 2 * 2), x_inv if value is None else value * x_inv)
-    share("xs", 2, xs_peers, lambda peer: x_coef.at[lax.rem(peer, half)], x_coef_in, xs_me)
-    x_coef_in[xs_me] = x_coef[pair]
+        x_coef[0, q] = value[:half]
+        x_coef[1, q] = value[half:]
+    x_two_coef[core] = x_coef[core]
+    share("xs", 2, mate, x_coef.at[other], x_two_coef.at[core])
+
+    y_local()
+
+    arrived(2, x_two_coef.at[0])
+    left_a, right_a, shared_a, left2_a, right2_a, shared2_a = (x_two_coef[0, q] for q in range(6))
+    left_b, right_b, shared_b, left2_b, right2_b, shared2_b = (x_two_coef[1, q] for q in range(6))
+    meet = 1.0 / (1.0 - right_a * left_b)
+    last_low, last_high = meet * shared_a, meet * right_a * shared_b
+    first_low, first_high = meet * left_b * shared_a, meet * shared_b
+    x_meet[0] = meet
+    for q, value in enumerate((last_low, last_high, first_low, first_high)):
+        x_meet[q + 1] = value
+
+    def joined(p0a, pna, p0b, pnb):
+        return (
+            p0a + shared_a * (meet * (p0b + left_b * pna)),
+            pnb + shared_b * (meet * (pna + right_a * p0b)),
+        )
+
+    first_from_low, _ = joined(
+        left2_a + shared2_a * first_low, shared2_a + right2_a * first_low,
+        left2_b * last_low, shared2_b * last_low,
+    )
+    first_from_high, last_from_high = joined(
+        shared2_a * first_high, right2_a * first_high,
+        left2_b * last_high + shared2_b, shared2_b * last_high + right2_b,
+    )
+    merged = (
+        left_a + shared_a * first_low, right_b + shared_b * last_high, shared_a * first_high,
+        first_from_low, last_from_high, first_from_high,
+    )
+    for q, value in enumerate(merged):
+        x_chip_coef[chip, q] = value
+    share("xs", 3, ring_peers, x_chip_coef.at[chip], x_chip_coef.at[chip])
 
     names = {"b": 0, "a1": 1, "a2": 2, "c1": 3, "c2": 4, "d": 5, "g": 6}
-    arrived(0, y_coef)
+    arrived(0, others(y_coef))
 
     def y_store(name, j, value):
         y_fac[names[name], j] = value
 
     reduced_factors(n_pl, lambda j: (y_coef[j, 0], y_coef[j, 1], y_coef[j, 2]), y_store)
-    y_local()
     y_finish(1, y_ends)
 
     p0 = pn = q0 = qn = jnp.zeros((nz, LANES), jnp.float32)
@@ -321,66 +349,101 @@
         q0 = q0 + x_second2[step(i)] * value
         qn = qn + x_first2[step(i)] * value
     for q, value in enumerate((p0, pn, q0, qn)):
-        halves(x_ends, ((), 2 * q), value)
-    share("xs", 3, xs_peers, lambda peer: x_ends.at[lax.rem(peer, half)], x_ends_in, xs_me)
-    x_ends_in[xs_me] = x_ends[pair]
-
-    arrived(2, x_coef_in)
+        x_ends[0, q] = value[:half]
+        x_ends[1, q] = value[half:]
+    share("xs", 4, mate, x_ends.at[other], x_two.at[core])
+    x_two[core] = x_ends[core]
+
+    x_solve(lambda i: plane[step(i)], into(x_part))
+
+    arrived(4, x_two.at[0])
+    left_a, right_a, shared_a, left2_a, right2_a, shared2_a = (x_two_coef[0, q] for q in range(6))
+    left_b, right_b, shared_b, left2_b, right2_b, shared2_b = (x_two_coef[1, q] for q in range(6))
+    meet, last_low, last_high, first_low, first_high = (x_meet[q] for q in range(5))
+
+    def border(p0b, pna):
+        return meet * (pna + right_a * p0b), meet * (p0b + left_b * pna)
+
+    def ends_again(last_a, first_b, low, high):
+        p0a, pna = x_two[0, 2] + shared2_a * first_b, x_two[0, 3] + right2_a * first_b
+        p0b, pnb = x_two[1, 2] + left2_b * last_a, x_two[1, 3] + shared2_b * last_a
+        if low is not None:
+            p0a, pna = p0a + left2_a * low, pna + shared2_a * low
+            p0b, pnb = p0b + shared2_b * high, pnb + right2_b * high
+        return p0a, pna, p0b, pnb
+
+    last_a, first_b = border(x_two[1, 0], x_two[0, 1])
+    x_chip[chip, 0] = x_two[0, 0] + shared_a * first_b
+    x_chip[chip, 1] = x_two[1, 1] + shared_b * last_a
+    p0a, pna, p0b, pnb = ends_again(last_a, first_b, None, None)
+    last2, first2 = border(p0b, pna)
+    x_chip[chip, 2] = p0a + shared_a * first2
+    x_chip[chip, 3] = pnb + shared_b * last2
+    share("xs", 5, ring_peers, x_chip.at[chip], x_chip.at[chip])
+
+    arrived(3, others(x_chip_coef))
 
     def x_store(name, j, value):
         x_fac[names[name], j] = value
 
-    def coef(j, q):
-        return x_coef_in[j, q // 2, q % 2 * 2:q % 2 * 2 + 2]
-
-    reduced_factors(n_xs, lambda j: (coef(j, 0), coef(j, 1), coef(j, 2)), x_store)
-    x_solve(lambda i: plane[step(i)], into(x_part))
-
-    arrived(3, x_ends_in)
+    reduced_factors(
+        chips, lambda j: (x_chip_coef[j, 0], x_chip_coef[j, 1], x_chip_coef[j, 2]), x_store
+    )
+    x_solve(lambda i: x_part[step(i)], into(x_part))
+
+    arrived(5, others(x_chip))
 
     def fac(name, j):
         return x_fac[names[name], j]
 
     def x_reduced(ends):
-        a = c = jnp.zeros((2, LANES), jnp.float32)
+        a = c = jnp.zeros((half, LANES), jnp.float32)
         lefts, rights = [a], [c]
-        for j in range(n_xs):
-            k = n_xs - 1 - j
+        for j in range(chips):
+            k = chips - 1 - j
             a = ends[j][1] + fac("a2", j) * ends[j][0] + fac("a1", j) * a
             c = ends[k][0] + fac("c2", k) * ends[k][1] + fac("c1", k) * c
             lefts.append(a)
             rights.append(c)
         rights = rights[::-1]
-        lows = [(lefts[j] + fac("b", j) * rights[j]) * fac("g", j) for j in range(n_xs)]
+        lows = [(lefts[j] + fac("b", j) * rights[j]) * fac("g", j) for j in range(chips)]
         highs = [
-            (rights[j + 1] + fac("d", j + 1) * lefts[j + 1]) * fac("g", j + 1) for j in range(n_xs)
+            (rights[j + 1] + fac("d", j + 1) * lefts[j + 1]) * fac("g", j + 1) for j in range(chips)
         ]
         return lows, highs
 
-    def end(j, q):
-        return x_ends_in[j, 2 * q:2 * q + 2]
-
-    lows, highs = x_reduced([(end(j, 0), end(j, 1)) for j in range(n_xs)])
+    lows, highs = x_reduced([(x_chip[j, 0], x_chip[j, 1]) for j in range(chips)])
     again = []
-    for j in range(n_xs):
-        left, right, shared = coef(j, 3), coef(j, 4), coef(j, 5)
+    for j in range(chips):
+        left, right, shared = (x_chip_coef[j, q] for q in range(3, 6))
         again.append(
             (
-                end(j, 2) + left * lows[j] + shared * highs[j],
-                end(j, 3) + shared * lows[j] + right * highs[j],
+                x_chip[j, 2] + left * lows[j] + shared * highs[j],
+                x_chip[j, 3] + shared * lows[j] + right * highs[j],
             )
         )
     lows2, highs2 = x_reduced(again)
-    for j in range(n_xs):
+    for j in range(chips):
         for q, value in enumerate((lows[j], highs[j], lows2[j], highs2[j])):
-            x_back[j, 2 * q:2 * q + 2] = value * coef(j, 2)
-    share("xs", 4, near_peers, lambda peer: x_back.at[peer], x_back_in, pair)
-    x_back_in[pair] = x_back[xs_me]
-
-    x_solve(lambda i: x_part[step(i)], into(x_part))
-    arrived(4, x_back_in)
+            x_outside[j, q] = value
+    low, high, low2, high2 = (x_outside[chip, q] for q in range(4))
+    last_a, first_b = border(x_two[1, 0], x_two[0, 1])
+    last_a = last_a + last_low * low + last_high * high
+    first_b = first_b + first_low * low + first_high * high
+    p0a, pna, p0b, pnb = ends_again(last_a, first_b, low, high)
+    last2, first2 = border(p0b, pna)
+    last2 = last2 + last_low * low2 + last_high * high2
+    first2 = first2 + first_low * low2 + first_high * high2
+    for q, value in enumerate((low, first_b, low2, first2)):
+        x_back[0, q] = value
+    for q, value in enumerate((last_a, high, last2, high2)):
+        x_back[1, q] = value
+    share("xs", 6, mate, x_back.at[other], x_back_in.at[core])
+    x_back_in[core] = x_back[core]
+
+    arrived(6, x_back_in.at[0])
     low1, high1, low2, high2 = (
-        jnp.concatenate([x_back_in[:, 2 * q], x_back_in[:, 2 * q + 1]], axis=0) for q in range(4)
+        jnp.concatenate([x_back_in[0, q], x_back_in[1, q]], axis=0) * x_inv for q in range(4)
     )
     for i in range(nx):
         plane[step(i)] = (
@@ -391,27 +454,29 @@
             + x_phi[step(i)] * high2
         )
 
-    y_send(5, y_ends2)
+    y_send(7, y_ends2)
     y_local()
-    y_finish(5, y_ends2)
+    y_finish(7, y_ends2)
 
     def to_out(z, value):
         out_ref[level(z)] = value
 
     z_solve(lambda z: plane[level(z)], to_out)
 
-    arrived(0, y_coef, send_sem)
-    arrived(1, y_ends, send_sem)
-    arrived(2, x_coef_in, send_sem)
-    arrived(3, x_ends_in, send_sem)
-    arrived(4, x_back_in, send_sem)
-    arrived(5, y_ends2, send_sem)
+    for slot, landing in enumerate(
+        (
+            others(y_coef), others(y_ends), x_two_coef.at[0], others(x_chip_coef),
+            x_two.at[0], others(x_chip), x_back_in.at[0], others(y_ends2),
+        )
+    ):
+        arrived(slot, landing, send_sem)
 
 
 def shards(n_pl, n_xs, source, eastward_rate, northward_rate, vertical_rate, amplitude):
     nx, nz, ny = source.shape
     lines = nx * nz
     blocks = lines // LANES
+    chips, half = n_xs // 2, nz // 2
     flat = lambda array: pltpu.with_memory_space_constraint(array.reshape(lines, ny), pltpu.HBM)
     field = pltpu.VMEM((lines, LANES), jnp.float32)
     column = pltpu.VMEM((nz, nx, LANES), jnp.float32)
@@ -431,18 +496,22 @@
             vmem(n_pl, 3, blocks, LANES),
             vmem(n_pl, 2, blocks, LANES),
             vmem(n_pl, 2, blocks, LANES),
-            vmem(n_xs // 2, 3, 4, LANES),
-            vmem(n_xs, 3, 4, LANES),
-            vmem(n_xs // 2, 8, LANES),
-            vmem(n_xs, 8, LANES),
-            vmem(n_xs, 8, LANES),
-            vmem(n_xs // 2, 8, LANES),
+            vmem(2, 6, half, LANES),
+            vmem(2, 6, half, LANES),
+            vmem(chips, 6, half, LANES),
+            vmem(2, 4, half, LANES),
+            vmem(2, 4, half, LANES),
+            vmem(chips, 4, half, LANES),
+            vmem(chips, 4, half, LANES),
+            vmem(2, 4, half, LANES),
+            vmem(2, 4, half, LANES),
+            vmem(5, half, LANES),
             vmem(7, n_pl + 1, blocks, LANES),
             vmem(2, n_pl + 1, blocks, LANES),
-            vmem(7, n_xs + 1, 2, LANES),
+            vmem(7, chips + 1, half, LANES),
             pltpu.SemaphoreType.DMA((4,)),
-            pltpu.SemaphoreType.DMA((6,)),
-            pltpu.SemaphoreType.DMA((6,)),
+            pltpu.SemaphoreType.DMA((8,)),
+            pltpu.SemaphoreType.DMA((8,)),
         ],
         compiler_params=pltpu.CompilerParams(
             collective_id=0, has_side_effects=True, vmem_limit_bytes=40 * 1024 * 1024

time: 29.7 us -> 28.5 us (0.960)
  Pallas kernels: 28.8 us -> 27.6 us
    pallas_call x1, Pallas kernels: 28.8 us -> 27.6 us  [shards(): pl.pallas_call(functools.partial(kernel, nx, nz, n_pl, n_xs), out_shape=j...]
where the time goes in v3:
time: 28.5 us; the launch traced here: 28.4 us
  Pallas kernels  27.6 us (97%)
  other arithmetic  0.74 us (3%)
    pallas_call x1, Pallas kernels, shards(): pl.pallas_call(functools.partial(kernel, nx, nz, n_pl, n_xs), out_shape=j...  27.6 us
    mul x1, other arithmetic, shards(): return amplitude * second.reshape(nx, nz, ny)  0.74 us

profile of v3, /device:TPU:1, one launch (start us, length us, event | category | flops | bytes accessed | tf_op | source)
XLA Modules:
  0.0 28.4 jit_solution(17093050146982662411)
XLA Ops:
  0.0 0.0 copy-start
  0.0 27.6 %adi.1 = f32[512,128]{1,0:T(8,128)S(1)} custom-call(f32[512,128]{1,0:T(8,128)} %bitcast.6, f32[512,128]{1,0:T(8,128)} %bitcast.7, f32[512,128]{1,0:T(8,128)} %bitcast.8, f32[512,128]{1,0:T(8,128)} %bitcast.9), custom_call_target="tpu_custom_call" | custom-call | tf_op jit(solution)/shard_map/adi/pallas_call | solution.py:484
  27.6 0.0 copy-done
  27.7 0.7 %mul.3 = f32[32,16,128]{2,1,0:T(8,128)} multiply(f32[32,16,128]{2,1,0:T(8,128)S(1)} %copy-done, f32[32,16,128]{2,1,0:T(8,128)S(1)} %bitcast.5) | non-fusion elementwise | flops 65536 | bytes 786432 | tf_op jit(solution)/shard_map/mul | solution.py:521
Async XLA Ops:
  0.0 27.6 %copy-start = (f32[32,16,128]{2,1,0:T(8,128)S(1)}, f32[32,16,128]{2,1,0:T(8,128)}, u32[]{:S(2)}) copy-start(f32[32,16,128]{2,1,0:T(8,128)} %param.9) | copy-start | bytes 786436

commit v4 on v3

--- a/solution.py
+++ b/solution.py
@@ -10,6 +10,8 @@
 
 MESH = pl.DeviceIdType.MESH
 LANES = 128
+Y_PITCH = LANES + 8
+Z_SPARE = 8
 HIGHEST = lax.Precision.HIGHEST
 
 
@@ -45,25 +47,30 @@
         store("g", j, one / (one - before * d))
 
 
-def running(count, first, second, value, phi, psi, keep, emit):
-    total = None
-    for i in reversed(range(count)):
-        term = second(i) * value(i)
-        if total is None:
-            total = jnp.zeros_like(term)
-        keep(i, total)
-        total = total + term
-    total = jnp.zeros_like(total)
-    for i in range(count):
-        total = total + first(i) * value(i)
-        emit(i, psi(i) * total + phi(i) * keep(i))
+def running(count, first, second, value, phi, psi, scale, keep, emit):
+    total = [None]
+
+    def down(i):
+        if i == count - 1:
+            total[0] = jnp.zeros_like(scale)
+        keep(i, total[0])
+        total[0] = total[0] + second(i) * value(i)
+
+    def up(i):
+        if i == 0:
+            total[0] = jnp.zeros_like(scale)
+        total[0] = total[0] + first(i) * value(i)
+        emit(i, scale * (psi(i) * total[0] + phi(i) * keep(i)))
+
+    downs = [functools.partial(down, i) for i in reversed(range(count))]
+    return downs + [functools.partial(up, i) for i in range(count)]
 
 
 def kernel(
     nx, nz, n_pl, n_xs,
     source_hbm, vertical_hbm, north_hbm, east_hbm, out_ref,
     source, vertical, north, east,
-    z_phi, z_psi, z_first, z_second,
+    z_phi, z_psi, z_first, z_second, z_rate, z_hold,
     y_rate, y_phi, y_psi, y_first, y_second, y_value, y_part,
     x_phi, x_psi, x_phi2, x_psi2, x_first, x_second, x_first2, x_second2,
     x_part, x_part2, plane, hold,
@@ -73,7 +80,17 @@
 ):
     lines = nx * nz
     blocks = lines // LANES
+    pitch, wide = nz + Z_SPARE, LANES // nz
     pl_me, xs_me = lax.axis_index("pl"), lax.axis_index("xs")
+
+    loads = []
+    for slot, (hbm, vmem) in enumerate(
+        ((north_hbm, north), (vertical_hbm, vertical), (source_hbm, source), (east_hbm, east))
+    ):
+        vmem = vmem.at[:, pl.ds(0, nz)] if len(vmem.shape) == 3 else vmem
+        copy = pltpu.make_async_copy(hbm, vmem, load_sem.at[slot])
+        copy.start()
+        loads.append(copy)
 
     side, chips, half = math.isqrt(n_pl), n_xs // 2, nz // 2
     pl_row, pl_col = pl_me // side, lax.rem(pl_me, side)
@@ -94,14 +111,6 @@
     for axis, peers in (("pl", pl_peers), ("xs", ring_peers + mate)):
         for peer in peers:
             pl.semaphore_signal(barrier, 1, device_id={axis: peer}, device_id_type=MESH)
-
-    loads = []
-    for slot, (hbm, vmem) in enumerate(
-        ((north_hbm, north), (vertical_hbm, vertical), (source_hbm, source), (east_hbm, east))
-    ):
-        copy = pltpu.make_async_copy(hbm, vmem, load_sem.at[slot])
-        copy.start()
-        loads.append(copy)
 
     def share(axis, slot, peers, source_ref, landing_ref):
         for peer in peers:
@@ -122,97 +131,117 @@
         return landing.at[pl.ds(0, landing.shape[0] - 1)]
 
     def rows(b):
-        return pl.ds(b * LANES, LANES)
+        return pl.ds(b * Y_PITCH, LANES)
 
     def across(y):
-        return pl.ds(y, blocks, stride=LANES)
-
-    loads[0].wait()
-    for b in range(blocks):
-        y_rate[rows(b)] = (1.0 / north[rows(b)]).T
-
-    def y_sweep(i, carry):
-        phi, phi_step, psi, psi_step = carry
-        y_phi[across(i)] = phi
-        y_psi[across(LANES - 1 - i)] = psi
-        phi_step = phi_step + phi * y_rate[across(i)]
-        psi_step = psi_step + psi * y_rate[across(LANES - 1 - i)]
-        return phi + phi_step, phi_step, psi + psi_step, psi_step
-
-    unit = jnp.ones((blocks, LANES), jnp.float32)
-    y_phi_end = lax.fori_loop(0, LANES, y_sweep, (unit, unit, unit, unit), unroll=8)[0]
-    y_inv = 1.0 / y_phi_end
-    hold[pl.ds(0, blocks)] = y_inv
-    for b in range(blocks):
-        inv = hold[b:b + 1]
-        scaled = y_rate[rows(b)] * inv
-        y_first[rows(b)] = y_phi[rows(b)] * scaled
-        y_second[rows(b)] = y_psi[rows(b)] * scaled
-    y_coef[pl_me, 0] = y_psi[across(0)] * y_inv
-    y_coef[pl_me, 1] = y_phi[across(LANES - 1)] * y_inv
-    y_coef[pl_me, 2] = y_inv
-
-    pl.semaphore_wait(barrier, n_pl + chips - 1)
-    share("pl", 0, pl_peers, y_coef.at[pl_me], y_coef.at[pl_me])
+        return pl.ds(y, blocks, stride=Y_PITCH)
 
     def level(z):
-        return pl.ds(z, nx, stride=nz)
-
-    loads[1].wait()
-    phi = jnp.ones((nx, LANES), jnp.float32)
-    phi_step = psi = psi_step = phi
-    for z in range(nz):
+        return pl.ds(z, nx, stride=pitch)
+
+    def plane_step(i):
+        return pl.ds(i * pitch, nz)
+
+    z_state = [jnp.ones((nx, LANES), jnp.float32)] * 4
+    z_steps = []
+
+    def z_invert(z):
+        z_rate[z] = 1.0 / vertical[:, z]
+
+    def z_sweep(z):
+        phi, phi_step, psi, psi_step = z_state
         back = nz - 1 - z
-        up, down = 1.0 / vertical[level(z)], 1.0 / vertical[level(back)]
         z_phi[z] = phi
         z_psi[back] = psi
-        z_first[z] = phi * up
-        z_second[back] = psi * down
-        phi_step = phi_step + phi * up
-        psi_step = psi_step + psi * down
-        phi = phi + phi_step
-        psi = psi + psi_step
-    z_inv = 1.0 / phi
-    for z in range(nz):
-        z_first[z] = z_first[z] * z_inv
-        z_second[z] = z_second[z] * z_inv
-
-    def z_solve(read, write):
+        phi_flux, psi_flux = phi * z_rate[z], psi * z_rate[back]
+        z_first[z] = phi_flux
+        z_second[back] = psi_flux
+        phi_step = phi_step + phi_flux
+        psi_step = psi_step + psi_flux
+        z_state[:] = [phi + phi_step, phi_step, psi + psi_step, psi_step]
+
+    def z_solve(z_inv, read, write):
         def keep(z, value=None):
             if value is None:
                 return x_part2[pl.ds(z * nx, nx)]
             x_part2[pl.ds(z * nx, nx)] = value
 
-        running(nz, lambda z: z_first[z], lambda z: z_second[z], read, lambda z: z_phi[z], lambda z: z_psi[z], keep, write)
-
-    loads[2].wait()
-
-    def to_plane(z, value):
-        plane[level(z)] = value
-
-    z_solve(lambda z: source[level(z)], to_plane)
+        return running(
+            nz, lambda z: z_first[z], lambda z: z_second[z], read, lambda z: z_phi[z], lambda z: z_psi[z],
+            z_inv, keep, write,
+        )
+
+    def z_first_solve():
+        z_hold[...] = 1.0 / z_state[0]
+
+        def to_plane(z, value):
+            plane[level(z)] = value
+
+        z_steps.extend(z_solve(z_hold[...], lambda z: source[:, z], to_plane))
+        z_steps.extend(functools.partial(y_turn, b) for b in range(blocks))
+
+    def y_turn(b):
+        y_value[rows(b)] = jnp.concatenate(
+            [plane[plane_step(b * wide + i)] for i in range(wide)], axis=0
+        ).T
+
+    for z in range(nz // 2):
+        for at in (z, nz - 1 - z):
+            z_steps.append(functools.partial(z_invert, at))
+    z_steps.extend(functools.partial(z_sweep, z) for z in range(nz))
+    z_steps.append(z_first_solve)
+
+    for copy in loads[:3]:
+        copy.wait()
+    for b in range(blocks):
+        y_rate[rows(b)] = (1.0 / north[b * LANES:(b + 1) * LANES]).T
+
+    unit = jnp.ones((blocks, LANES), jnp.float32)
+    phi, phi_step, psi, psi_step = unit, unit, unit, unit
+    for i in range(LANES):
+        back = LANES - 1 - i
+        y_phi[across(i)] = phi
+        y_psi[across(back)] = psi
+        phi_flux, psi_flux = phi * y_rate[across(i)], psi * y_rate[across(back)]
+        y_first[across(i)] = phi_flux
+        y_second[across(back)] = psi_flux
+        phi_step = phi_step + phi_flux
+        psi_step = psi_step + psi_flux
+        phi = phi + phi_step
+        psi = psi + psi_step
+        if z_steps and i % 16 < 10:
+            z_steps.pop(0)()
+    while z_steps:
+        z_steps.pop(0)()
+    y_inv = 1.0 / phi
+    hold[pl.ds(2 * blocks, blocks)] = y_inv
+    y_coef[pl_me, 0] = y_psi[across(0)] * y_inv
+    y_coef[pl_me, 1] = y_phi[across(LANES - 1)] * y_inv
+    y_coef[pl_me, 2] = y_inv
 
     low = lax.broadcasted_iota(jnp.int32, (LANES, LANES), 0)
     high = lax.broadcasted_iota(jnp.int32, (LANES, LANES), 1)
     upto = jnp.where(high <= low, 1.0, 0.0)
     beyond = jnp.where(high > low, 1.0, 0.0)
 
-    def y_send(slot, ends):
+    def y_inv_row(b):
+        return hold[2 * blocks + b:2 * blocks + b + 1]
+
+    def y_ends_of(ends):
         for b in range(blocks):
-            value = plane[rows(b)].T
+            value = y_value[rows(b)]
             second = y_second[rows(b)] * value
             first = y_first[rows(b)] * value
             y_value[rows(b)] = first
             y_part[rows(b)] = second
-            ends[pl_me, 0, b:b + 1] = jnp.sum(second, axis=0, keepdims=True)
-            ends[pl_me, 1, b:b + 1] = jnp.sum(first, axis=0, keepdims=True)
-        share("pl", slot, pl_peers, ends.at[pl_me], ends.at[pl_me])
+            ends[pl_me, 0, b:b + 1] = jnp.sum(second, axis=0, keepdims=True) * y_inv_row(b)
+            ends[pl_me, 1, b:b + 1] = jnp.sum(first, axis=0, keepdims=True) * y_inv_row(b)
 
     def y_local():
         for b in range(blocks):
             below = jnp.dot(upto, y_value[rows(b)], precision=HIGHEST, preferred_element_type=jnp.float32)
             above = jnp.dot(beyond, y_part[rows(b)], precision=HIGHEST, preferred_element_type=jnp.float32)
-            y_part[rows(b)] = y_psi[rows(b)] * below + y_phi[rows(b)] * above
+            y_part[rows(b)] = (y_psi[rows(b)] * below + y_phi[rows(b)] * above) * y_inv_row(b)
 
     def y_finish(slot, ends):
         arrived(slot, others(ends))
@@ -238,9 +267,11 @@
                 + y_psi[rows(b)] * hold[b:b + 1]
                 + y_phi[rows(b)] * hold[blocks + b:blocks + b + 1]
             )
-            plane[rows(b)] = solved.T
-
-    y_send(1, y_ends)
+            solved = solved.T
+            for i in range(wide):
+                plane[plane_step(b * wide + i)] = solved[i * nz:(i + 1) * nz]
+
+    y_ends_of(y_ends)
 
     def step(i):
         return pl.ds(i * nz, nz)
@@ -248,31 +279,33 @@
     loads[3].wait()
     phi = jnp.ones((nz, LANES), jnp.float32)
     phi_step = psi = psi_step = phi
+    for i in range(nx // 2):
+        for at in (i, nx - 1 - i):
+            east[step(at)] = 1.0 / east[step(at)]
     for i in range(nx):
         back = nx - 1 - i
-        up, down = 1.0 / east[step(i)], 1.0 / east[step(back)]
         x_phi[step(i)] = phi
         x_psi[step(back)] = psi
-        x_first[step(i)] = phi * up
-        x_second[step(back)] = psi * down
-        phi_step = phi_step + phi * up
-        psi_step = psi_step + psi * down
+        phi_flux, psi_flux = phi * east[step(i)], psi * east[step(back)]
+        x_first[step(i)] = phi_flux
+        x_second[step(back)] = psi_flux
+        phi_step = phi_step + phi_flux
+        psi_step = psi_step + psi_flux
         phi = phi + phi_step
         psi = psi + psi_step
     x_inv = 1.0 / phi
-    for i in range(nx):
-        x_first[step(i)] = x_first[step(i)] * x_inv
-        x_second[step(i)] = x_second[step(i)] * x_inv
-
-    def x_solve(read, write):
+
+    def x_solve(read, write, spare=None):
+        spare = x_part2 if spare is None else spare
+
         def keep(i, value=None):
             if value is None:
-                return x_part2[step(i)]
-            x_part2[step(i)] = value
-
-        running(
+                return spare[step(i)]
+            spare[step(i)] = value
+
+        return running(
             nx, lambda i: x_first[step(i)], lambda i: x_second[step(i)], read,
-            lambda i: x_phi[step(i)], lambda i: x_psi[step(i)], keep, write,
+            lambda i: x_phi[step(i)], lambda i: x_psi[step(i)], x_inv, keep, write,
         )
 
     def into(ref):
@@ -281,12 +314,15 @@
 
         return write
 
-    x_solve(lambda i: x_phi[step(i)], into(x_phi2))
-    x_solve(lambda i: x_psi[step(i)], into(x_psi2))
+    for one, two in zip(
+        x_solve(lambda i: x_phi[step(i)], into(x_phi2)),
+        x_solve(lambda i: x_psi[step(i)], into(x_psi2), x_part),
+    ):
+        one()
+        two()
     for i in range(nx):
-        scaled = x_inv * (1.0 / east[step(i)])
-        x_first2[step(i)] = x_phi2[step(i)] * scaled
-        x_second2[step(i)] = x_psi2[step(i)] * scaled
+        x_first2[step(i)] = x_phi2[step(i)] * east[step(i)]
+        x_second2[step(i)] = x_psi2[step(i)] * east[step(i)]
     last = step(nx - 1)
     coefficients = (
         x_psi[step(0)] * x_inv, x_phi[last] * x_inv, x_inv,
@@ -296,7 +332,10 @@
         x_coef[0, q] = value[:half]
         x_coef[1, q] = value[half:]
     x_two_coef[core] = x_coef[core]
+    pl.semaphore_wait(barrier, n_pl + chips - 1)
     share("xs", 2, mate, x_coef.at[other], x_two_coef.at[core])
+    share("pl", 0, pl_peers, y_coef.at[pl_me], y_coef.at[pl_me])
+    share("pl", 1, pl_peers, y_ends.at[pl_me], y_ends.at[pl_me])
 
     y_local()
 
@@ -343,18 +382,19 @@
 
     p0 = pn = q0 = qn = jnp.zeros((nz, LANES), jnp.float32)
     for i in range(nx):
-        value = plane[step(i)]
+        value = plane[plane_step(i)]
         p0 = p0 + x_second[step(i)] * value
         pn = pn + x_first[step(i)] * value
         q0 = q0 + x_second2[step(i)] * value
         qn = qn + x_first2[step(i)] * value
     for q, value in enumerate((p0, pn, q0, qn)):
-        x_ends[0, q] = value[:half]
-        x_ends[1, q] = value[half:]
+        x_ends[0, q] = value[:half] * x_inv[:half]
+        x_ends[1, q] = value[half:] * x_inv[half:]
     share("xs", 4, mate, x_ends.at[other], x_two.at[core])
     x_two[core] = x_ends[core]
 
-    x_solve(lambda i: plane[step(i)], into(x_part))
+    for run in x_solve(lambda i: plane[plane_step(i)], into(x_part)):
+        run()
 
     arrived(4, x_two.at[0])
     left_a, right_a, shared_a, left2_a, right2_a, shared2_a = (x_two_coef[0, q] for q in range(6))
@@ -389,7 +429,8 @@
     reduced_factors(
         chips, lambda j: (x_chip_coef[j, 0], x_chip_coef[j, 1], x_chip_coef[j, 2]), x_store
     )
-    x_solve(lambda i: x_part[step(i)], into(x_part))
+    for run in x_solve(lambda i: x_part[step(i)], into(x_part)):
+        run()
 
     arrived(5, others(x_chip))
 
@@ -446,7 +487,7 @@
         jnp.concatenate([x_back_in[0, q], x_back_in[1, q]], axis=0) * x_inv for q in range(4)
     )
     for i in range(nx):
-        plane[step(i)] = (
+        plane[plane_step(i)] = (
             x_part[step(i)]
             + x_psi2[step(i)] * low1
             + x_phi2[step(i)] * high1
@@ -454,14 +495,18 @@
             + x_phi[step(i)] * high2
         )
 
-    y_send(7, y_ends2)
+    for b in range(blocks):
+        y_turn(b)
+    y_ends_of(y_ends2)
+    share("pl", 7, pl_peers, y_ends2.at[pl_me], y_ends2.at[pl_me])
     y_local()
     y_finish(7, y_ends2)
 
     def to_out(z, value):
-        out_ref[level(z)] = value
-
-    z_solve(lambda z: plane[level(z)], to_out)
+        out_ref[pl.ds(z, nx, stride=nz)] = value
+
+    for run in z_solve(z_hold[...], lambda z: plane[level(z)], to_out):
+        run()
 
     for slot, landing in enumerate(
         (
@@ -477,8 +522,11 @@
     lines = nx * nz
     blocks = lines // LANES
     chips, half = n_xs // 2, nz // 2
-    flat = lambda array: pltpu.with_memory_space_constraint(array.reshape(lines, ny), pltpu.HBM)
+    here = lambda array: pltpu.with_memory_space_constraint(array, pltpu.HBM)
+    flat = lambda array: here(array.reshape(lines, ny))
     field = pltpu.VMEM((lines, LANES), jnp.float32)
+    padded = pltpu.VMEM((nx, nz + Z_SPARE, LANES), jnp.float32)
+    turned = pltpu.VMEM((blocks * Y_PITCH, LANES), jnp.float32)
     column = pltpu.VMEM((nz, nx, LANES), jnp.float32)
     vmem = lambda *shape: pltpu.VMEM(shape, jnp.float32)
     second = pl.pallas_call(
@@ -486,12 +534,14 @@
         out_shape=jax.ShapeDtypeStruct((lines, ny), jnp.float32),
         in_specs=[pl.BlockSpec(memory_space=pltpu.HBM)] * 4,
         out_specs=pl.BlockSpec(memory_space=pltpu.VMEM),
-        scratch_shapes=[field] * 4
-        + [column] * 4
-        + [field] * 7
+        scratch_shapes=[padded, padded, field, field]
+        + [column] * 5
+        + [vmem(nx, LANES)]
+        + [turned] * 7
         + [field] * 8
-        + [field] * 3
-        + [vmem(2 * blocks, LANES)]
+        + [field] * 2
+        + [vmem(nx * (nz + Z_SPARE), LANES)]
+        + [vmem(3 * blocks, LANES)]
         + [
             vmem(n_pl, 3, blocks, LANES),
             vmem(n_pl, 2, blocks, LANES),
@@ -517,7 +567,7 @@
             collective_id=0, has_side_effects=True, vmem_limit_bytes=40 * 1024 * 1024
         ),
         name="adi",
-    )(flat(source), flat(vertical_rate), flat(northward_rate), flat(eastward_rate))
+    )(here(source), here(vertical_rate), flat(northward_rate), flat(eastward_rate))
     return amplitude * second.reshape(nx, nz, ny)
 
 

time: 28.5 us -> 28.1 us (0.986)
  Pallas kernels: 27.6 us -> 27.2 us
    pallas_call x1, Pallas kernels: 27.6 us -> 27.2 us  [shards(): pl.pallas_call(functools.partial(kernel, nx, nz, n_pl, n_xs), out_shape=j...]
where the time goes in v4:
time: 28.1 us; the launch traced here: 28 us
  Pallas kernels  27.2 us (97%)
  other arithmetic  0.74 us (3%)
    pallas_call x1, Pallas kernels, shards(): pl.pallas_call(functools.partial(kernel, nx, nz, n_pl, n_xs), out_shape=j...  27.2 us
    mul x1, other arithmetic, shards(): return amplitude * second.reshape(nx, nz, ny)  0.74 us

profile of v4, /device:TPU:1, one launch (start us, length us, event | category | flops | bytes accessed | tf_op | source)
XLA Modules:
  0.0 28.0 jit_solution(11206682520215158659)
XLA Ops:
  0.0 0.0 copy-start
  0.0 27.2 %adi.1 = f32[512,128]{1,0:T(8,128)S(1)} custom-call(f32[32,16,128]{2,1,0:T(8,128)} %source_hbm.1, f32[32,16,128]{2,1,0:T(8,128)} %vertical_hbm.1, f32[512,128]{1,0:T(8,128)} %bitcast.4, f32[512,128]{1,0:T(8,128)} %bitcast.5), custom_call_target="tpu_custom_call" | custom-call | tf_op jit(solution)/shard_map/adi/pallas_call | solution.py:532
  27.3 0.0 copy-done
  27.3 0.7 %mul.3 = f32[32,16,128]{2,1,0:T(8,128)} multiply(f32[32,16,128]{2,1,0:T(8,128)S(1)} %copy-done, f32[32,16,128]{2,1,0:T(8,128)S(1)} %bitcast.3) | non-fusion elementwise | flops 65536 | bytes 786432 | tf_op jit(solution)/shard_map/mul | solution.py:571
Async XLA Ops:
  0.0 27.3 %copy-start = (f32[32,16,128]{2,1,0:T(8,128)S(1)}, f32[32,16,128]{2,1,0:T(8,128)}, u32[]{:S(2)}) copy-start(f32[32,16,128]{2,1,0:T(8,128)} %param.9) | copy-start | bytes 786436

commit v5 on v4

--- a/solution.py
+++ b/solution.py
@@ -160,15 +160,17 @@
         psi_step = psi_step + psi_flux
         z_state[:] = [phi + phi_step, phi_step, psi + psi_step, psi_step]
 
-    def z_solve(z_inv, read, write):
+    def z_solve(z_inv, read, write, start=0, count=nx):
+        group = pl.ds(start, count)
+
         def keep(z, value=None):
             if value is None:
-                return x_part2[pl.ds(z * nx, nx)]
-            x_part2[pl.ds(z * nx, nx)] = value
+                return x_part2[pl.ds(z * nx + start, count)]
+            x_part2[pl.ds(z * nx + start, count)] = value
 
         return running(
-            nz, lambda z: z_first[z], lambda z: z_second[z], read, lambda z: z_phi[z], lambda z: z_psi[z],
-            z_inv, keep, write,
+            nz, lambda z: z_first[z, group], lambda z: z_second[z, group], read,
+            lambda z: z_phi[z, group], lambda z: z_psi[z, group], z_inv, keep, write,
         )
 
     def z_first_solve():
@@ -243,7 +245,7 @@
             above = jnp.dot(beyond, y_part[rows(b)], precision=HIGHEST, preferred_element_type=jnp.float32)
             y_part[rows(b)] = (y_psi[rows(b)] * below + y_phi[rows(b)] * above) * y_inv_row(b)
 
-    def y_finish(slot, ends):
+    def y_finish(slot, ends, consume):
         arrived(slot, others(ends))
         a = c = jnp.zeros((blocks, LANES), jnp.float32)
         y_scan[0, 0] = a
@@ -270,6 +272,7 @@
             solved = solved.T
             for i in range(wide):
                 plane[plane_step(b * wide + i)] = solved[i * nz:(i + 1) * nz]
+            consume(b, solved)
 
     y_ends_of(y_ends)
 
@@ -378,16 +381,17 @@
         y_fac[names[name], j] = value
 
     reduced_factors(n_pl, lambda j: (y_coef[j, 0], y_coef[j, 1], y_coef[j, 2]), y_store)
-    y_finish(1, y_ends)
-
-    p0 = pn = q0 = qn = jnp.zeros((nz, LANES), jnp.float32)
-    for i in range(nx):
-        value = plane[plane_step(i)]
-        p0 = p0 + x_second[step(i)] * value
-        pn = pn + x_first[step(i)] * value
-        q0 = q0 + x_second2[step(i)] * value
-        qn = qn + x_first2[step(i)] * value
-    for q, value in enumerate((p0, pn, q0, qn)):
+    sums = [jnp.zeros((nz, LANES), jnp.float32)] * 4
+
+    def add_ends(b, solved):
+        for i in range(wide):
+            at, value = step(b * wide + i), solved[i * nz:(i + 1) * nz]
+            for q, weight in enumerate((x_second, x_first, x_second2, x_first2)):
+                sums[q] = sums[q] + weight[at] * value
+
+    y_finish(1, y_ends, add_ends)
+
+    for q, value in enumerate(sums):
         x_ends[0, q] = value[:half] * x_inv[:half]
         x_ends[1, q] = value[half:] * x_inv[half:]
     share("xs", 4, mate, x_ends.at[other], x_two.at[core])
@@ -486,27 +490,32 @@
     low1, high1, low2, high2 = (
         jnp.concatenate([x_back_in[0, q], x_back_in[1, q]], axis=0) * x_inv for q in range(4)
     )
-    for i in range(nx):
-        plane[plane_step(i)] = (
-            x_part[step(i)]
-            + x_psi2[step(i)] * low1
-            + x_phi2[step(i)] * high1
-            + x_psi[step(i)] * low2
-            + x_phi[step(i)] * high2
-        )
-
     for b in range(blocks):
-        y_turn(b)
+        pieces = [
+            x_part[at]
+            + x_psi2[at] * low1
+            + x_phi2[at] * high1
+            + x_psi[at] * low2
+            + x_phi[at] * high2
+            for at in (step(b * wide + i) for i in range(wide))
+        ]
+        y_value[rows(b)] = jnp.concatenate(pieces, axis=0).T
     y_ends_of(y_ends2)
     share("pl", 7, pl_peers, y_ends2.at[pl_me], y_ends2.at[pl_me])
     y_local()
-    y_finish(7, y_ends2)
-
-    def to_out(z, value):
-        out_ref[pl.ds(z, nx, stride=nz)] = value
-
-    for run in z_solve(z_hold[...], lambda z: plane[level(z)], to_out):
-        run()
+    def finish_z(b, solved):
+        start = b * wide
+
+        def read(z):
+            return plane[pl.ds(start * pitch + z, wide, stride=pitch)]
+
+        def write(z, value):
+            out_ref[pl.ds(start * nz + z, wide, stride=nz)] = value
+
+        for run in z_solve(z_hold[start:start + wide], read, write, start, wide):
+            run()
+
+    y_finish(7, y_ends2, finish_z)
 
     for slot, landing in enumerate(
         (

time: 28.1 us -> 28.1 us (level)
  no operation moved by 1% of the time
where the time goes in v5:
time: 28.1 us; the launch traced here: 28 us
  Pallas kernels  27.2 us (97%)
  other arithmetic  0.74 us (3%)
    pallas_call x1, Pallas kernels, shards(): pl.pallas_call(functools.partial(kernel, nx, nz, n_pl, n_xs), out_shape=j...  27.2 us
    mul x1, other arithmetic, shards(): return amplitude * second.reshape(nx, nz, ny)  0.74 us

profile of v5, /device:TPU:1, one launch (start us, length us, event | category | flops | bytes accessed | tf_op | source)
XLA Modules:
  0.0 28.0 jit_solution(3128738195537737294)
XLA Ops:
  0.0 0.0 copy-start
  0.0 27.2 %adi.1 = f32[512,128]{1,0:T(8,128)S(1)} custom-call(f32[32,16,128]{2,1,0:T(8,128)} %source_hbm.1, f32[32,16,128]{2,1,0:T(8,128)} %vertical_hbm.1, f32[512,128]{1,0:T(8,128)} %bitcast.4, f32[512,128]{1,0:T(8,128)} %bitcast.5), custom_call_target="tpu_custom_call" | custom-call | tf_op jit(solution)/shard_map/adi/pallas_call | solution.py:541
  27.3 0.0 copy-done
  27.3 0.7 %mul.3 = f32[32,16,128]{2,1,0:T(8,128)} multiply(f32[32,16,128]{2,1,0:T(8,128)S(1)} %copy-done, f32[32,16,128]{2,1,0:T(8,128)S(1)} %bitcast.3) | non-fusion elementwise | flops 65536 | bytes 786432 | tf_op jit(solution)/shard_map/mul | solution.py:580
Async XLA Ops:
  0.0 27.3 %copy-start = (f32[32,16,128]{2,1,0:T(8,128)S(1)}, f32[32,16,128]{2,1,0:T(8,128)}, u32[]{:S(2)}) copy-start(f32[32,16,128]{2,1,0:T(8,128)} %param.9) | copy-start | bytes 786436

commit v6 on v4

--- a/solution.py
+++ b/solution.py
@@ -437,7 +437,7 @@
     def fac(name, j):
         return x_fac[names[name], j]
 
-    def x_reduced(ends):
+    def x_reduced(ends, only_here=False):
         a = c = jnp.zeros((half, LANES), jnp.float32)
         lefts, rights = [a], [c]
         for j in range(chips):
@@ -447,6 +447,15 @@
             lefts.append(a)
             rights.append(c)
         rights = rights[::-1]
+        if only_here:
+            for j in range(chips + 1):
+                x_outside[j, 0] = lefts[j]
+                x_outside[j, 1] = rights[j]
+            here, after = chip, chip + 1
+            return (
+                (x_outside[here, 0] + x_fac[0, here] * x_outside[here, 1]) * x_fac[6, here],
+                (x_outside[after, 1] + x_fac[5, after] * x_outside[after, 0]) * x_fac[6, after],
+            )
         lows = [(lefts[j] + fac("b", j) * rights[j]) * fac("g", j) for j in range(chips)]
         highs = [
             (rights[j + 1] + fac("d", j + 1) * lefts[j + 1]) * fac("g", j + 1) for j in range(chips)
@@ -463,11 +472,11 @@
                 x_chip[j, 3] + shared * lows[j] + right * highs[j],
             )
         )
-    lows2, highs2 = x_reduced(again)
     for j in range(chips):
-        for q, value in enumerate((lows[j], highs[j], lows2[j], highs2[j])):
-            x_outside[j, q] = value
-    low, high, low2, high2 = (x_outside[chip, q] for q in range(4))
+        x_outside[j, 2] = lows[j]
+        x_outside[j, 3] = highs[j]
+    low2, high2 = x_reduced(again, only_here=True)
+    low, high = x_outside[chip, 2], x_outside[chip, 3]
     last_a, first_b = border(x_two[1, 0], x_two[0, 1])
     last_a = last_a + last_low * low + last_high * high
     first_b = first_b + first_low * low + first_high * high
@@ -552,7 +561,7 @@
             vmem(2, 4, half, LANES),
             vmem(2, 4, half, LANES),
             vmem(chips, 4, half, LANES),
-            vmem(chips, 4, half, LANES),
+            vmem(chips + 1, 4, half, LANES),
             vmem(2, 4, half, LANES),
             vmem(2, 4, half, LANES),
             vmem(5, half, LANES),

time: 28.1 us -> 28.1 us (level)
  no operation moved by 1% of the time
where the time goes in v6:
time: 28.1 us; the launch traced here: 28 us
  Pallas kernels  27.2 us (97%)
  other arithmetic  0.74 us (3%)
    pallas_call x1, Pallas kernels, shards(): pl.pallas_call(functools.partial(kernel, nx, nz, n_pl, n_xs), out_shape=j...  27.2 us
    mul x1, other arithmetic, shards(): return amplitude * second.reshape(nx, nz, ny)  0.74 us

profile of v6, /device:TPU:1, one launch (start us, length us, event | category | flops | bytes accessed | tf_op | source)
XLA Modules:
  0.0 28.0 jit_solution(10880636905770284531)
XLA Ops:
  0.0 0.0 copy-start
  0.0 27.2 %adi.1 = f32[512,128]{1,0:T(8,128)S(1)} custom-call(f32[32,16,128]{2,1,0:T(8,128)} %source_hbm.1, f32[32,16,128]{2,1,0:T(8,128)} %vertical_hbm.1, f32[512,128]{1,0:T(8,128)} %bitcast.4, f32[512,128]{1,0:T(8,128)} %bitcast.5), custom_call_target="tpu_custom_call" | custom-call | tf_op jit(solution)/shard_map/adi/pallas_call | solution.py:541
  27.3 0.0 copy-done
  27.3 0.7 %mul.3 = f32[32,16,128]{2,1,0:T(8,128)} multiply(f32[32,16,128]{2,1,0:T(8,128)S(1)} %copy-done, f32[32,16,128]{2,1,0:T(8,128)S(1)} %bitcast.3) | non-fusion elementwise | flops 65536 | bytes 786432 | tf_op jit(solution)/shard_map/mul | solution.py:580
Async XLA Ops:
  0.0 27.3 %copy-start = (f32[32,16,128]{2,1,0:T(8,128)S(1)}, f32[32,16,128]{2,1,0:T(8,128)}, u32[]{:S(2)}) copy-start(f32[32,16,128]{2,1,0:T(8,128)} %param.9) | copy-start | bytes 786436

commit v7 on v4

--- a/solution.py
+++ b/solution.py
@@ -108,7 +108,9 @@
     mate = [chip * 2 + other]
 
     barrier = pltpu.get_barrier_semaphore()
-    for axis, peers in (("pl", pl_peers), ("xs", ring_peers + mate)):
+    for axis, peers in (
+        ("pl", pl_peers[:5]), ("xs", ring_peers[:3]), ("pl", pl_peers[5:]), ("xs", ring_peers[3:] + mate),
+    ):
         for peer in peers:
             pl.semaphore_signal(barrier, 1, device_id={axis: peer}, device_id_type=MESH)
 

time: 28.1 us -> 28.1 us (level)
  no operation moved by 1% of the time
where the time goes in v7:
time: 28.1 us; the launch traced here: 28 us
  Pallas kernels  27.2 us (97%)
  other arithmetic  0.74 us (3%)
    pallas_call x1, Pallas kernels, shards(): pl.pallas_call(functools.partial(kernel, nx, nz, n_pl, n_xs), out_shape=j...  27.2 us
    mul x1, other arithmetic, shards(): return amplitude * second.reshape(nx, nz, ny)  0.74 us

profile of v7, /device:TPU:1, one launch (start us, length us, event | category | flops | bytes accessed | tf_op | source)
XLA Modules:
  0.0 28.0 jit_solution(3691361577511533344)
XLA Ops:
  0.0 0.0 copy-start
  0.0 27.2 %adi.1 = f32[512,128]{1,0:T(8,128)S(1)} custom-call(f32[32,16,128]{2,1,0:T(8,128)} %source_hbm.1, f32[32,16,128]{2,1,0:T(8,128)} %vertical_hbm.1, f32[512,128]{1,0:T(8,128)} %bitcast.4, f32[512,128]{1,0:T(8,128)} %bitcast.5), custom_call_target="tpu_custom_call" | custom-call | tf_op jit(solution)/shard_map/adi/pallas_call | solution.py:534
  27.2 0.0 copy-done
  27.2 0.7 %mul.3 = f32[32,16,128]{2,1,0:T(8,128)} multiply(f32[32,16,128]{2,1,0:T(8,128)S(1)} %copy-done, f32[32,16,128]{2,1,0:T(8,128)S(1)} %bitcast.3) | non-fusion elementwise | flops 65536 | bytes 786432 | tf_op jit(solution)/shard_map/mul | solution.py:573
Async XLA Ops:
  0.0 27.2 %copy-start = (f32[32,16,128]{2,1,0:T(8,128)S(1)}, f32[32,16,128]{2,1,0:T(8,128)}, u32[]{:S(2)}) copy-start(f32[32,16,128]{2,1,0:T(8,128)} %param.9) | copy-start | bytes 786436
